TPU v7x, 32 devices: a whole 2x2x4 slice. The times are simulated.
32 devices in a mesh: groups: 2 (over y), seq: 4 (over z), chan: 2 (over x), sub: 2 (over core).
Axes of the slice: x: 2, y: 2, z: 4, core: 2. Of those that a mesh axis runs over, the one named last changes fastest.
Arguments:
- x_in: bfloat16 [1024, 8192], P(('groups', 'seq'), ('chan', 'sub')), parts along dimension 0, may hold values from -36 to 36
- b_in: bfloat16 [1024, 4, 256], P(('groups', 'seq'), 'chan'), parts along dimension 0, may hold values from -6 to 6
- c_in: bfloat16 [1024, 4, 256], P(('groups', 'seq'), 'chan'), parts along dimension 0, may hold values from -0.375 to 0.375
- step_size: float32 [1024, 128], P(('groups', 'seq'), ('chan', 'sub')), parts along dimension 0, may hold values from 0.02 to 0.2
- log_decay: float32 [1024, 128], P(('groups', 'seq'), ('chan', 'sub')), parts along dimension 0, may hold values from -1 to 0, as said below
- skip: float32 [128], P(('chan', 'sub')), may hold values from 0.5 to 1.5
- gate_in: bfloat16 [1024, 8192], P(('groups', 'seq'), ('chan', 'sub')), parts along dimension 0, may hold values from -6 to 6
- norm_gain: float32 [8192], P(('chan', 'sub')), may hold values from 0.1 to 1.9
- walsh_sign: int32 [8192], P(('chan', 'sub')), may hold values from 0 to 1
- channel_shift_power: int32 [8192], P(('chan', 'sub')), may hold values from -1 to 3
- out_weight: bfloat16 [8192, 4096], P(('chan', 'sub'), 'seq'), may hold values from -0.0625 to 0.0625
Outputs:
- projected: bfloat16 [1024, 4096], P(('groups', 'seq', 'chan', 'sub')), parts along dimension 0
There are 2 independent parts, one for each index of `groups`. A program takes and returns all parts, laid end to end along the dimension named above; an argument that names none is the same for every part. Nothing has to cross between parts.
Inputs may be any that keep to these rules, and one draw needn't show every extreme that they name: `log_decay`: every entry is negative.
All inputs are finite; a program needn't handle non-finite values.
Results may differ from a plain program's by a relative error of at most 0.024.
Values may be sent and summed in bfloat16 or wider, within the bound.
A program may use at most 128 MiB of HBM per device.

v0:
```python
import functools
import math

import jax
import jax.numpy as jnp
from jax import lax
from jax.experimental import pallas as pl
from jax.experimental.pallas import tpu as pltpu
from jax.sharding import PartitionSpec as P

LOCAL_HEADS = 128
P_SIZE = 64
G = 4
NORM_HEADS = 16


norm_eps = 1e-05
clip_level = 4.0
expo_levels = (-1, 0, 1, 2, 3)
lanes = 128
MESH = pl.DeviceIdType.MESH


def partner_2(block, axis, bit):
    count = lax.axis_size(axis)
    route = []
    for low in range(count):
        high = low | 1 << bit
        if high != low and high < count:
            route += [(low, high), (high, low)]
    return lax.ppermute(block, axis, route)


def power_two(expo, sign_flip):
    result = jnp.zeros(expo.shape, jnp.float32)
    for level in expo_levels:
        result = result + jnp.where(
            expo == level, jnp.float32(2.0 ** (sign_flip * level)), jnp.float32(0.0)
        )
    return result


def sylvester(order):
    indices = jnp.arange(order, dtype=jnp.int32)
    oddness_flag = jnp.zeros((order, order), jnp.int32)
    for bit_index in range(order.bit_length() - 1):
        stride = 2**bit_index
        oddness_flag = oddness_flag + indices[:, None] // stride % 2 * (
            indices[None, :] // stride % 2
        )
    return (1 - 2 * (oddness_flag % 2)).astype(jnp.bfloat16)


def halves(value):
    upper = value.astype(jnp.bfloat16)
    return upper, (value - upper.astype(jnp.float32)).astype(jnp.bfloat16)


def dot32(left, right):
    return jnp.dot(left, right, preferred_element_type=jnp.float32)


def earlier_kernel(
    n, tile, x_ref, b_ref, total_ref, c_ref, y_ref, x_in, b_in, total_in, run, send, recv
):
    me = lax.axis_index("seq")
    barrier = pltpu.get_barrier_semaphore()

    @pl.loop(1, n)
    def _(d):
        pl.semaphore_signal(
            barrier, inc=1, device_id={"seq": lax.rem(me + d, n)}, device_id_type=MESH
        )

    pl.semaphore_wait(barrier, n - 1)

    def copies(d):
        target = {"seq": lax.rem(me + d, n)}
        pairs = ((b_ref, b_in), (total_ref, total_in), (x_ref, x_in))
        return [
            pltpu.make_async_remote_copy(
                src_ref=source,
                dst_ref=landing.at[d],
                send_sem=send.at[d, i],
                recv_sem=recv.at[d, i],
                device_id=target,
                device_id_type=MESH,
            )
            for i, (source, landing) in enumerate(pairs)
        ]

    @pl.loop(1, n)
    def _(d):
        @pl.when(me + d < n)
        def _():
            for copy in copies(d):
                copy.start()

    y_ref[...] = jnp.zeros_like(y_ref)
    run[...] = jnp.zeros_like(run)

    @pl.loop(1, n)
    def _(d):
        @pl.when(me >= d)
        def _():
            for copy in copies(d):
                copy.wait_recv()
            mixing = lax.dot_general(
                c_ref[...],
                b_in[d],
                (((1,), (1,)), ((), ())),
                preferred_element_type=jnp.float32,
            )
            upper, lower = halves(mixing)

            @pl.loop(0, y_ref.shape[1] // tile)
            def _(i):
                at = pl.ds(pl.multiple_of(i * tile, tile), tile)
                block = x_in[d, :, at]
                y_ref[:, at] += (dot32(upper, block) + dot32(lower, block)) * jnp.exp(run[:, at])

            run[...] += total_in[d]

    @pl.loop(1, n)
    def _(d):
        @pl.when(me + d < n)
        def _():
            for copy in copies(d):
                copy.wait_send()


def earlier_blocks(x_end, b_group, total, c_group):
    n = lax.axis_size("seq")
    rows, width = x_end.shape
    vmem = pl.BlockSpec(memory_space=pltpu.VMEM)
    return pl.pallas_call(
        functools.partial(earlier_kernel, n, min(512, width)),
        out_shape=jax.ShapeDtypeStruct((rows, width), jnp.float32),
        in_specs=[vmem] * 4,
        out_specs=vmem,
        scratch_shapes=[
            pltpu.VMEM((n, rows, width), jnp.bfloat16),
            pltpu.VMEM((n, rows, b_group.shape[1]), jnp.bfloat16),
            pltpu.VMEM((n, 1, width), jnp.float32),
            pltpu.VMEM((1, width), jnp.float32),
            pltpu.SemaphoreType.DMA((n, 3)),
            pltpu.SemaphoreType.DMA((n, 3)),
        ],
        compiler_params=pltpu.CompilerParams(
            collective_id=0, has_side_effects=True, vmem_limit_bytes=48 * 2**20
        ),
    )(x_end, b_group, total, c_group)


def rotate_kernel(factor, mixed_ref, table_ref, up_ref, down_ref, out_ref):
    count = mixed_ref.shape[1] // lanes
    parts = [mixed_ref[:, i * lanes : (i + 1) * lanes] for i in range(count)]
    span = 1
    while span < count:
        for i in range(count):
            if not i & span:
                a, b = parts[i], parts[i + span]
                parts[i], parts[i + span] = a + b, a - b
        span *= 2
    table = table_ref[...]
    for i in range(count):
        at = slice(i * lanes, (i + 1) * lanes)
        upper, lower = halves(parts[i])
        rotated = (dot32(upper, table) + dot32(lower, table)) * factor
        quant = jnp.clip(rotated * up_ref[:, at], -clip_level, clip_level).astype(jnp.bfloat16)
        out_ref[:, at] = (quant.astype(jnp.float32) * down_ref[:, at]).astype(jnp.bfloat16)


def rotate(mixed, up, down):
    vmem = pl.BlockSpec(memory_space=pltpu.VMEM)
    return pl.pallas_call(
        functools.partial(rotate_kernel, 1.0 / math.sqrt(LOCAL_HEADS * P_SIZE)),
        out_shape=jax.ShapeDtypeStruct(mixed.shape, jnp.bfloat16),
        in_specs=[vmem] * 4,
        out_specs=vmem,
    )(mixed, sylvester(lanes), up[None, :], down[None, :])


def project_kernel(
    n,
    n_chan,
    n_sub,
    tile,
    scaled_ref,
    weight_hbm,
    out_ref,
    weight,
    slots,
    partial,
    slabs,
    summed,
    landed,
    local_sem,
    g_send,
    g_recv,
    s_send,
    s_recv,
    f_send,
    f_recv,
):
    me = lax.axis_index("seq")
    peers = n_chan * n_sub
    here = lax.axis_index("chan") * n_sub + lax.axis_index("sub")
    rows, feats = out_ref.shape[0], weight.shape[1]

    def slab_device(e):
        other = lax.rem(here + e, peers)
        return other, {"chan": other // n_sub, "sub": lax.rem(other, n_sub)}

    fetch = pltpu.make_async_copy(weight_hbm, weight, local_sem.at[0])
    own = pltpu.make_async_copy(scaled_ref, slots.at[0], local_sem.at[1])
    fetch.start()
    own.start()
    barrier = pltpu.get_barrier_semaphore()

    @pl.loop(1, n)
    def _(d):
        pl.semaphore_signal(
            barrier, inc=1, device_id={"seq": lax.rem(me + d, n)}, device_id_type=MESH
        )

    @pl.loop(1, peers)
    def _(e):
        pl.semaphore_signal(barrier, inc=1, device_id=slab_device(e)[1], device_id_type=MESH)

    pl.semaphore_wait(barrier, n - 1 + peers - 1)

    def offset(s):
        return jnp.where(lax.rem(s, 2) == 1, (s + 1) // 2, lax.rem(n - s // 2, n))

    def gather(d):
        return pltpu.make_async_remote_copy(
            src_ref=scaled_ref,
            dst_ref=slots.at[d],
            send_sem=g_send.at[d],
            recv_sem=g_recv.at[d],
            device_id={"seq": lax.rem(me + d, n)},
            device_id_type=MESH,
        )

    def slab(d, e):
        other, device = slab_device(e)
        return pltpu.make_async_remote_copy(
            src_ref=partial.at[d, pl.ds(pl.multiple_of(other * rows, rows), rows)],
            dst_ref=slabs.at[d, e],
            send_sem=s_send.at[d, e],
            recv_sem=s_recv.at[d, e],
            device_id=device,
            device_id_type=MESH,
        )

    def finish(d):
        return pltpu.make_async_remote_copy(
            src_ref=summed.at[d],
            dst_ref=landed.at[d],
            send_sem=f_send.at[d],
            recv_sem=f_recv.at[d],
            device_id={"seq": lax.rem(me - d + n, n)},
            device_id_type=MESH,
        )

    @pl.loop(1, n)
    def _(s):
        gather(offset(s)).start()

    own.wait()
    fetch.wait()

    def reduce_block(s):
        d = offset(s)

        @pl.loop(1, peers)
        def _(e):
            slab(d, e).wait_recv()

        mine = pl.ds(pl.multiple_of(here * rows, rows), rows)
        total = partial[d, mine, :].astype(jnp.float32)
        for e in range(1, peers):
            total = total + slabs[d, e].astype(jnp.float32)
        summed[d] = total.astype(jnp.bfloat16)

        @pl.when(d > 0)
        def _():
            finish(d).start()

    @pl.loop(0, n)
    def _(s):
        d = offset(s)

        @pl.when(s > 0)
        def _():
            gather(d).wait_recv()

        @pl.loop(0, feats // tile)
        def _(i):
            at = pl.ds(pl.multiple_of(i * tile, tile), tile)
            partial[d, :, at] = dot32(slots[d], weight[:, at]).astype(jnp.bfloat16)

        @pl.loop(1, peers)
        def _(e):
            slab(d, e).start()

        @pl.when(s > 0)
        def _():
            reduce_block(s - 1)

    reduce_block(n - 1)

    def columns(d):
        return pl.ds(pl.multiple_of(lax.rem(me + d, n) * feats, feats), feats)

    out_ref[:, columns(0)] = summed[0]

    @pl.loop(1, n)
    def _(s):
        d = offset(s)
        finish(d).wait_recv()
        out_ref[:, columns(d)] = landed[d]

    @pl.loop(1, n)
    def _(d):
        gather(d).wait_send()
        finish(d).wait_send()

    @pl.loop(0, n)
    def _(d):
        @pl.loop(1, peers)
        def _(e):
            slab(d, e).wait_send()


def project(scaled, weight):
    n, n_chan, n_sub = (lax.axis_size(axis) for axis in ("seq", "chan", "sub"))
    peers = n_chan * n_sub
    rows, depth = scaled.shape
    feats = weight.shape[1]
    own_rows = rows // peers
    vmem = pl.BlockSpec(memory_space=pltpu.VMEM)
    dma = pltpu.SemaphoreType.DMA
    return pl.pallas_call(
        functools.partial(project_kernel, n, n_chan, n_sub, min(256, feats)),
        out_shape=jax.ShapeDtypeStruct((own_rows, n * feats), jnp.bfloat16),
        in_specs=[vmem, pl.BlockSpec(memory_space=pl.ANY)],
        out_specs=vmem,
        scratch_shapes=[
            pltpu.VMEM(weight.shape, jnp.bfloat16),
            pltpu.VMEM((n, rows, depth), jnp.bfloat16),
            pltpu.VMEM((n, rows, feats), jnp.bfloat16),
            pltpu.VMEM((n, peers, own_rows, feats), jnp.bfloat16),
            pltpu.VMEM((n, own_rows, feats), jnp.bfloat16),
            pltpu.VMEM((n, own_rows, feats), jnp.bfloat16),
            dma((2,)),
            dma((n,)),
            dma((n,)),
            dma((n, peers)),
            dma((n, peers)),
            dma((n,)),
            dma((n,)),
        ],
        compiler_params=pltpu.CompilerParams(
            collective_id=1, has_side_effects=True, vmem_limit_bytes=48 * 2**20
        ),
    )(scaled, weight)


def body(
    x_in,
    b_in,
    c_in,
    step_size,
    log_decay,
    skip,
    gate_in,
    norm_gain,
    walsh_sign,
    channel_shift_power,
    out_weight,
):
    highest = lax.Precision.HIGHEST
    tok_rows, chan_width = x_in.shape
    head_local = step_size.shape[1]
    head_group = LOCAL_HEADS // G
    sub_index = lax.axis_index("sub")
    group_local = sub_index * head_local // head_group
    b_group = lax.dynamic_slice_in_dim(b_in, group_local, 1, 1)[:, 0, :]
    c_group = lax.dynamic_slice_in_dim(c_in, group_local, 1, 1)[:, 0, :]
    x_heads = x_in.astype(jnp.float32).reshape(tok_rows, head_local, P_SIZE)
    weighted = x_heads * step_size[:, :, None]
    cumul = jnp.cumsum(log_decay, axis=0)
    inner = jnp.dot(c_group, b_group.T, preferred_element_type=jnp.float32)
    differ = cumul[:, None, :] - cumul[None, :, :]
    causal = (jnp.arange(tok_rows)[:, None] >= jnp.arange(tok_rows)[None, :])[:, :, None]
    ratio = jnp.where(causal, jnp.exp(jnp.where(causal, differ, 0.0)), 0.0)
    mixing = ratio * inner[:, :, None]
    y_diag = jnp.einsum("tuh,uhp->thp", mixing, weighted, precision=highest).reshape(
        tok_rows, chan_width
    )
    to_end = jnp.exp(cumul[-1][None, :] - cumul)
    x_end = (weighted * to_end[:, :, None]).reshape(tok_rows, chan_width).astype(jnp.bfloat16)
    total = jnp.repeat(cumul[-1], P_SIZE)[None, :]
    y_off = earlier_blocks(x_end, b_group, total, c_group) * jnp.repeat(
        jnp.exp(cumul), P_SIZE, axis=1
    )
    y_ssm = y_diag + y_off + (x_heads * skip[None, :, None]).reshape(tok_rows, chan_width)
    gated_pre = y_ssm * jax.nn.silu(gate_in.astype(jnp.float32))
    grouped = gated_pre.reshape(tok_rows, head_local // NORM_HEADS, NORM_HEADS * P_SIZE)
    mean_sq = jnp.mean(grouped * grouped, axis=2, keepdims=True)
    gated = (
        (grouped * lax.rsqrt(mean_sq + norm_eps)).reshape(tok_rows, chan_width) * norm_gain[None, :]
    ).astype(jnp.bfloat16)
    sign_value = jnp.where(walsh_sign == 1, 1.0, -1.0).astype(jnp.bfloat16)
    signed = gated * sign_value[None, :]
    partner = partner_2(signed, "sub", 0)
    own_float = signed.astype(jnp.float32)
    partner_float = partner.astype(jnp.float32)
    mixed = jnp.where(sub_index % 2 == 1, partner_float - own_float, own_float + partner_float)
    chan_index = lax.axis_index("chan")
    for bit_index in range(lax.axis_size("chan").bit_length() - 1):
        partner = partner_2(mixed.astype(jnp.bfloat16), "chan", bit_index).astype(mixed.dtype)
        chan_bit = chan_index // 2**bit_index % 2
        mixed = jnp.where(chan_bit == 1, partner - mixed, mixed + partner)
    scaled = rotate(mixed, power_two(channel_shift_power, 1), power_two(channel_shift_power, -1))
    return project(scaled, out_weight)


def solution(mesh):
    return jax.shard_map(
        body,
        mesh=mesh,
        in_specs=(
            P(("groups", "seq"), ("chan", "sub")),
            P(("groups", "seq"), "chan", None),
            P(("groups", "seq"), "chan", None),
            P(("groups", "seq"), ("chan", "sub")),
            P(("groups", "seq"), ("chan", "sub")),
            P(("chan", "sub")),
            P(("groups", "seq"), ("chan", "sub")),
            P(("chan", "sub")),
            P(("chan", "sub")),
            P(("chan", "sub")),
            P(("chan", "sub"), "seq"),
        ),
        out_specs=P(("groups", "seq", "chan", "sub"), None),
        check_vma=False,
    )
```

profile of v0, /device:TPU:0, one launch (start us, length us, event | category | flops | bytes accessed | tf_op | source)
XLA Modules:
  0.0 166.6 jit_solution(10029899541486020150)
XLA Ops:
  0.0 0.8 copy.44
  0.8 0.2 reduce_window_sum.11
  1.1 1.2 constant_dynamic-slice_fusion
  2.6 0.3 copy.51
  3.0 1.1 mul.186
  4.0 1.6 copy.49
  5.7 1.2 copy.43
  7.0 6.5 %fusion = f32[32,64,128]{2,1,0:T(8,128)} fusion(f32[128,128]{1,0:T(8,128)S(1)} %fusion.42, f32[128,32]{0,1:T(8,128)S(1)} %copy.45, f32[128,32,64]{0,2,1:T(8,128)} %bitcast.30, pred[128,128]{1,0:T(8,128)(4,1)S(1)} %iota_compare_fusion, f32[128,32]{0,1:T(8,128)S(1)} %copy-done.6), kind=kOutput, calls=%fused_computation | convolution fusion | flops 405012480 | bytes 2211840 | tf_op jit(solution)/shard_map/tuh,uhp->thp/dot_general | solution.py:400
  13.6 2.5 %copy.54 = f32[128,2048]{1,0:T(8,128)} copy(f32[128,2048]{0,1:T(8,128)} %bitcast.31) | data formatting | bytes 2097152 | tf_op jit(solution)/shard_map/reshape | solution.py:400
  16.2 1.1 broadcast_in_dim.103
  17.2 2.6 %copy.53 = f32[128,2048]{1,0:T(8,128)} copy(f32[128,2048]{0,1:T(8,128)} %bitcast.27) | data formatting | bytes 2097152 | tf_op jit(solution)/shard_map/reshape | solution.py:406
  19.9 0.2 multiply_convert_fusion.1.x_ref
  20.1 43.8 %shard_map.109 = f32[128,2048]{1,0:T(8,128)S(1)} custom-call(bf16[128,2048]{1,0:T(8,128)(2,1)S(1)} %multiply_convert_fusion.1.x_ref, bf16[128,256]{1,0:T(8,128)(2,1)S(1)} %bitcast.22, f32[1,2048]{1,0:T(1,128)S(1)} %broadcast_in_dim_reshape.3.total_ref, bf16[128,256]{1,0:T(8,128)(2,1)S(1)} %bitcast.24), custom_call_target="tpu_custom_call" | custom-call | tf_op jit(solution)/shard_map/pallas_call | solution.py:136
  63.9 1.5 fusion.39
  65.4 2.1 %mul.204 = f32[128,2,1024]{2,1,0:T(2,128)S(1)} reshape(f32[128,2048]{1,0:T(8,128)} %get-tuple-element.11) | data formatting | bytes 2097152 | tf_op jit(solution)/shard_map/mul | solution.py:412
  67.5 0.3 reduce_sum.9
  67.9 0.3 mul.205
  68.3 0.3 copy.59
  68.6 0.2 fusion.19
  69.0 0.6 fusion.30
  69.6 1.2 collective-permute-done
  70.8 0.2 fusion.18
  71.0 1.6 collective-permute-start.1
  72.6 0.6 fusion.27
  73.2 0.8 fusion.24.table_ref
  74.0 11.1 %collective-permute-done.1 = bf16[128,2048]{1,0:T(8,128)(2,1)S(1)} collective-permute-done((bf16[128,2048]{1,0:T(8,128)(2,1)S(1)}, bf16[128,2048]{1,0:T(8,128)(2,1)S(1)}, u32[]{:S(2)}, u32[]{:S(2)}) %collective-permute-start.1) | collective-permute-done | bytes 524320 | tf_op jit(solution)/shard_map/ppermute | solution.py:31
  85.0 1.3 fusion.11.mixed_ref
  86.3 2.7 %shard_map.110.scaled_ref = bf16[128,2048]{1,0:T(8,128)(2,1)} custom-call(f32[128,2048]{1,0:T(8,128)} %fusion.11.mixed_ref, bf16[128,128]{1,0:T(8,128)(2,1)} %fusion.24.table_ref, f32[1,2048]{1,0:T(1,128)} %bitcast.33, f32[1,2048]{1,0:T(1,128)} %bitcast.32), custom_call_target="tpu_custom_call" | custom-call | tf_op jit(solution)/shard_map/pallas_call | solution.py:176
  89.0 2.2 %copy-done = bf16[2048,1024]{1,0:T(8,128)(2,1)S(1)} copy-done((bf16[2048,1024]{1,0:T(8,128)(2,1)S(1)}, bf16[2048,1024]{1,0:T(8,128)(2,1)}, u32[]{:S(2)}) %copy-start) | copy-done | bytes 4194328
  91.2 1.0 copy-done.1
  92.3 73.6 %shard_map.111 = bf16[32,4096]{1,0:T(8,128)(2,1)S(1)} custom-call(bf16[128,2048]{1,0:T(8,128)(2,1)S(1)} %copy-done.1, bf16[2048,1024]{1,0:T(8,128)(2,1)S(1)} %copy-done), custom_call_target="tpu_custom_call" | custom-call | tf_op jit(solution)/shard_map/pallas_call | solution.py:345
  165.9 0.7 copy.66
  (41 shorter events, 0.9 us)
Async XLA Ops:
  1.1 1.8 %copy-start.6 = (f32[128,32]{0,1:T(8,128)S(1)}, f32[128,32]{0,1:T(8,128)}, u32[]{:S(2)}) copy-start(f32[128,32]{0,1:T(8,128)} %param.14) | copy-start | bytes 49156
  2.9 2.8 %copy-start.2 = (bf16[128,2048]{1,0:T(8,128)(2,1)S(1)}, bf16[128,2048]{1,0:T(8,128)(2,1)}, u32[]{:S(2)}) copy-start(bf16[128,2048]{1,0:T(8,128)(2,1)} %param.11) | copy-start | bytes 1572868
  16.1 3.7 %copy-start.10 = (f32[32]{0:T(128)S(1)}, f32[32]{0:T(128)}, u32[]{:S(2)}) copy-start(f32[32]{0:T(128)} %param.16) | copy-start | bytes 388
  19.9 44.0 %copy-start.3 = (f32[128,2048]{1,0:T(8,128)S(1)}, f32[128,2048]{1,0:T(8,128)}, u32[]{:S(2)}) copy-start(f32[128,2048]{1,0:T(8,128)} %copy.54) | copy-start | bytes 3145732
  19.9 44.0 %copy-start.4 = (f32[128,2048]{1,0:T(8,128)S(1)}, f32[128,2048]{1,0:T(8,128)}, u32[]{:S(2)}) copy-start(f32[128,2048]{1,0:T(8,128)} %copy.53) | copy-start | bytes 3145732
  19.9 44.0 %copy-start.5 = (bf16[128,2048]{1,0:T(8,128)(2,1)S(1)}, bf16[128,2048]{1,0:T(8,128)(2,1)}, u32[]{:S(2)}) copy-start(bf16[128,2048]{1,0:T(8,128)(2,1)} %param.17) | copy-start | bytes 1572868
  67.5 1.1 copy-start.8
  67.5 1.1 copy-start.7
  68.3 0.7 copy-start.9
  68.8 2.0 %collective-permute-start = (bf16[128,2048]{1,0:T(8,128)(2,1)S(1)}, bf16[128,2048]{1,0:T(8,128)(2,1)S(1)}, u32[]{:S(2)}, u32[]{:S(2)}) collective-permute-start(bf16[128,2048]{1,0:T(8,128)(2,1)S(1)} %fusion.19), channel_id=1, source_target_pairs={{0,1},{1,0},{2,3},{3,2},{4,5},{5,4},{6,7},{7,6},{8,9},{9,8},{10,11... | collective-permute-start | bytes 1572872 | tf_op jit(solution)/shard_map/ppermute | solution.py:31
  71.0 14.0 %collective-permute-start.1 = (bf16[128,2048]{1,0:T(8,128)(2,1)S(1)}, bf16[128,2048]{1,0:T(8,128)(2,1)S(1)}, u32[]{:S(2)}, u32[]{:S(2)}) collective-permute-start(bf16[128,2048]{1,0:T(8,128)(2,1)S(1)} %fusion.18), channel_id=1, source_target_pairs={{0,2},{2,0},{1,3},{3,1},{4,6},{6,4},{5,7},{7,5},{8,10},{10,8},{9,1... | collective-permute-start | bytes 1572872 | tf_op jit(solution)/shard_map/ppermute | solution.py:31
  89.0 2.2 %copy-start = (bf16[2048,1024]{1,0:T(8,128)(2,1)S(1)}, bf16[2048,1024]{1,0:T(8,128)(2,1)}, u32[]{:S(2)}) copy-start(bf16[2048,1024]{1,0:T(8,128)(2,1)} %weight_hbm.1) | copy-start | bytes 12582916
  91.2 1.0 copy-start.1
where the time goes:
time: 169 us; the launch traced here: 167 us
  Pallas kernels  120 us (71%)
  local copies, waits for them, and re-layouts  19.7 us (12%)
  waiting for transfers between devices  12.3 us (7%)
  matrix products  6.66 us (4%)
  other arithmetic  5.95 us (4%)
    pallas_call x1, Pallas kernels, project(): pl.pallas_call(functools.partial(project_kernel, n, n_chan, n_sub, min(25...  73.6 us
    pallas_call x1, Pallas kernels, earlier_blocks(): pl.pallas_call(functools.partial(earlier_kernel, n, min(512, width)), out...  43.8 us
    ppermute x2, waiting for transfers between devices, partner_2(): return lax.ppermute(block, axis, route)  12.3 us
    dot_general x1, matrix products, body(): jnp.einsum('tuh,uhp->thp', mixing, weighted, precision=highest)  6.55 us
    unnamed x27, local copies, waits for them, and re-layouts  5.15 us
  transfers between devices with their start and end apart: 2, of which 2 were waited for; matrix products, arithmetic and copies ran while one was open for 1% of the time, Pallas kernels for 0%

commit v1 on v0

--- a/solution.py
+++ b/solution.py
@@ -60,96 +60,82 @@
     return jnp.dot(left, right, preferred_element_type=jnp.float32)
 
 
-def earlier_kernel(
-    n, tile, x_ref, b_ref, total_ref, c_ref, y_ref, x_in, b_in, total_in, run, send, recv
+def carry_kernel(
+    n, tile, x_ref, bt_ref, total_ref, c_ref, y_ref, arrived, leaving, send, recv
 ):
     me = lax.axis_index("seq")
+    right, left = lax.rem(me + 1, n), lax.rem(me + n - 1, n)
     barrier = pltpu.get_barrier_semaphore()
-
-    @pl.loop(1, n)
-    def _(d):
-        pl.semaphore_signal(
-            barrier, inc=1, device_id={"seq": lax.rem(me + d, n)}, device_id_type=MESH
-        )
-
-    pl.semaphore_wait(barrier, n - 1)
-
-    def copies(d):
-        target = {"seq": lax.rem(me + d, n)}
-        pairs = ((b_ref, b_in), (total_ref, total_in), (x_ref, x_in))
-        return [
-            pltpu.make_async_remote_copy(
-                src_ref=source,
-                dst_ref=landing.at[d],
-                send_sem=send.at[d, i],
-                recv_sem=recv.at[d, i],
-                device_id=target,
-                device_id_type=MESH,
+    for near in (left, right):
+        pl.semaphore_signal(barrier, inc=1, device_id={"seq": near}, device_id_type=MESH)
+    pl.semaphore_wait(barrier, 2)
+
+    def copy(i):
+        return pltpu.make_async_remote_copy(
+            src_ref=leaving.at[i],
+            dst_ref=arrived.at[i],
+            send_sem=send.at[i],
+            recv_sem=recv.at[i],
+            device_id={"seq": right},
+            device_id_type=MESH,
+        )
+
+    @pl.loop(0, y_ref.shape[1] // tile)
+    def _(i):
+        at = pl.ds(pl.multiple_of(i * tile, tile), tile)
+        upper, lower = halves(x_ref[:, at])
+        own = dot32(bt_ref[...], upper) + dot32(bt_ref[...], lower)
+
+        @pl.when(me == 0)
+        def _():
+            leaving[i] = own.astype(jnp.bfloat16)
+            y_ref[:, at] = jnp.zeros((y_ref.shape[0], tile), jnp.float32)
+
+        @pl.when(me > 0)
+        def _():
+            copy(i).wait_recv()
+            state = arrived[i]
+            leaving[i] = (state.astype(jnp.float32) * jnp.exp(total_ref[:, at]) + own).astype(
+                jnp.bfloat16
             )
-            for i, (source, landing) in enumerate(pairs)
-        ]
-
-    @pl.loop(1, n)
-    def _(d):
-        @pl.when(me + d < n)
-        def _():
-            for copy in copies(d):
-                copy.start()
-
-    y_ref[...] = jnp.zeros_like(y_ref)
-    run[...] = jnp.zeros_like(run)
-
-    @pl.loop(1, n)
-    def _(d):
-        @pl.when(me >= d)
-        def _():
-            for copy in copies(d):
-                copy.wait_recv()
-            mixing = lax.dot_general(
-                c_ref[...],
-                b_in[d],
-                (((1,), (1,)), ((), ())),
-                preferred_element_type=jnp.float32,
-            )
-            upper, lower = halves(mixing)
-
-            @pl.loop(0, y_ref.shape[1] // tile)
-            def _(i):
-                at = pl.ds(pl.multiple_of(i * tile, tile), tile)
-                block = x_in[d, :, at]
-                y_ref[:, at] += (dot32(upper, block) + dot32(lower, block)) * jnp.exp(run[:, at])
-
-            run[...] += total_in[d]
-
-    @pl.loop(1, n)
-    def _(d):
-        @pl.when(me + d < n)
-        def _():
-            for copy in copies(d):
-                copy.wait_send()
-
-
-def earlier_blocks(x_end, b_group, total, c_group):
+
+        @pl.when(me + 1 < n)
+        def _():
+            copy(i).start()
+
+        @pl.when(me > 0)
+        def _():
+            y_ref[:, at] = dot32(c_ref[...], arrived[i])
+
+    @pl.when(me + 1 < n)
+    def _():
+        @pl.loop(0, y_ref.shape[1] // tile)
+        def _(i):
+            copy(i).wait_send()
+
+
+def carry(x_end, b_group, total, c_group):
     n = lax.axis_size("seq")
     rows, width = x_end.shape
+    tile = min(256, width)
+    tiles = width // tile
+    states = b_group.shape[1]
     vmem = pl.BlockSpec(memory_space=pltpu.VMEM)
     return pl.pallas_call(
-        functools.partial(earlier_kernel, n, min(512, width)),
+        functools.partial(carry_kernel, n, tile),
         out_shape=jax.ShapeDtypeStruct((rows, width), jnp.float32),
         in_specs=[vmem] * 4,
         out_specs=vmem,
         scratch_shapes=[
-            pltpu.VMEM((n, rows, width), jnp.bfloat16),
-            pltpu.VMEM((n, rows, b_group.shape[1]), jnp.bfloat16),
-            pltpu.VMEM((n, 1, width), jnp.float32),
-            pltpu.VMEM((1, width), jnp.float32),
-            pltpu.SemaphoreType.DMA((n, 3)),
-            pltpu.SemaphoreType.DMA((n, 3)),
+            pltpu.VMEM((tiles, states, tile), jnp.bfloat16),
+            pltpu.VMEM((tiles, states, tile), jnp.bfloat16),
+            pltpu.SemaphoreType.DMA((tiles,)),
+            pltpu.SemaphoreType.DMA((tiles,)),
         ],
         compiler_params=pltpu.CompilerParams(
             collective_id=0, has_side_effects=True, vmem_limit_bytes=48 * 2**20
         ),
-    )(x_end, b_group, total, c_group)
+    )(x_end, b_group.T, total, c_group)
 
 
 def rotate_kernel(factor, mixed_ref, table_ref, up_ref, down_ref, out_ref):
@@ -213,7 +199,7 @@
         return other, {"chan": other // n_sub, "sub": lax.rem(other, n_sub)}
 
     fetch = pltpu.make_async_copy(weight_hbm, weight, local_sem.at[0])
-    own = pltpu.make_async_copy(scaled_ref, slots.at[0], local_sem.at[1])
+    own = pltpu.make_async_copy(scaled_ref, slots.at[me], local_sem.at[1])
     fetch.start()
     own.start()
     barrier = pltpu.get_barrier_semaphore()
@@ -230,108 +216,127 @@
 
     pl.semaphore_wait(barrier, n - 1 + peers - 1)
 
-    def offset(s):
-        return jnp.where(lax.rem(s, 2) == 1, (s + 1) // 2, lax.rem(n - s // 2, n))
-
-    def gather(d):
+    def block_at(s):
+        return me + jnp.where(lax.rem(s, 2) == 1, -((s + 1) // 2), s // 2)
+
+    def hop(k, way):
         return pltpu.make_async_remote_copy(
-            src_ref=scaled_ref,
-            dst_ref=slots.at[d],
-            send_sem=g_send.at[d],
-            recv_sem=g_recv.at[d],
-            device_id={"seq": lax.rem(me + d, n)},
+            src_ref=slots.at[k],
+            dst_ref=slots.at[k],
+            send_sem=g_send.at[way, k],
+            recv_sem=g_recv.at[k],
+            device_id={"seq": lax.rem(me + (1 if way == 1 else n - 1), n)},
             device_id_type=MESH,
         )
 
-    def slab(d, e):
+    def slab(k, e):
         other, device = slab_device(e)
         return pltpu.make_async_remote_copy(
-            src_ref=partial.at[d, pl.ds(pl.multiple_of(other * rows, rows), rows)],
-            dst_ref=slabs.at[d, e],
-            send_sem=s_send.at[d, e],
-            recv_sem=s_recv.at[d, e],
+            src_ref=partial.at[k, pl.ds(pl.multiple_of(other * rows, rows), rows)],
+            dst_ref=slabs.at[k, e],
+            send_sem=s_send.at[k, e],
+            recv_sem=s_recv.at[k, e],
             device_id=device,
             device_id_type=MESH,
         )
 
-    def finish(d):
+    def finish(k, z):
         return pltpu.make_async_remote_copy(
-            src_ref=summed.at[d],
-            dst_ref=landed.at[d],
-            send_sem=f_send.at[d],
-            recv_sem=f_recv.at[d],
-            device_id={"seq": lax.rem(me - d + n, n)},
+            src_ref=summed.at[k],
+            dst_ref=landed.at[me],
+            send_sem=f_send.at[k],
+            recv_sem=f_recv.at[z],
+            device_id={"seq": k},
             device_id_type=MESH,
         )
 
-    @pl.loop(1, n)
-    def _(s):
-        gather(offset(s)).start()
+    def when_valid(s, act):
+        k = block_at(s)
+        pl.when(jnp.logical_and(k >= 0, k < n))(lambda: act(k))
 
     own.wait()
+
+    def pass_on(k):
+        @pl.when(jnp.logical_and(k <= me, me + 1 < n))
+        def _():
+            hop(k, 1).start()
+
+        @pl.when(jnp.logical_and(k >= me, me > 0))
+        def _():
+            hop(k, 0).start()
+
+    pass_on(me)
     fetch.wait()
 
-    def reduce_block(s):
-        d = offset(s)
-
-        @pl.loop(1, peers)
-        def _(e):
-            slab(d, e).wait_recv()
-
-        mine = pl.ds(pl.multiple_of(here * rows, rows), rows)
-        total = partial[d, mine, :].astype(jnp.float32)
-        for e in range(1, peers):
-            total = total + slabs[d, e].astype(jnp.float32)
-        summed[d] = total.astype(jnp.bfloat16)
-
-        @pl.when(d > 0)
-        def _():
-            finish(d).start()
-
-    @pl.loop(0, n)
-    def _(s):
-        d = offset(s)
-
-        @pl.when(s > 0)
-        def _():
-            gather(d).wait_recv()
+    def project_block(k):
+        @pl.when(k != me)
+        def _():
+            hop(k, 1).wait_recv()
+            pass_on(k)
 
         @pl.loop(0, feats // tile)
         def _(i):
             at = pl.ds(pl.multiple_of(i * tile, tile), tile)
-            partial[d, :, at] = dot32(slots[d], weight[:, at]).astype(jnp.bfloat16)
+            partial[k, :, at] = dot32(slots[k], weight[:, at]).astype(jnp.bfloat16)
 
         @pl.loop(1, peers)
         def _(e):
-            slab(d, e).start()
+            slab(k, e).start()
+
+    def reduce_block(k):
+        @pl.loop(1, peers)
+        def _(e):
+            slab(k, e).wait_recv()
+
+        mine = pl.ds(pl.multiple_of(here * rows, rows), rows)
+        total = partial[k, mine, :].astype(jnp.float32)
+        for e in range(1, peers):
+            total = total + slabs[k, e].astype(jnp.float32)
+        summed[k] = total.astype(jnp.bfloat16)
+
+        @pl.when(k != me)
+        def _():
+            finish(k, me).start()
+
+    @pl.loop(0, 2 * n - 1)
+    def _(s):
+        when_valid(s, project_block)
 
         @pl.when(s > 0)
         def _():
-            reduce_block(s - 1)
-
-    reduce_block(n - 1)
-
-    def columns(d):
-        return pl.ds(pl.multiple_of(lax.rem(me + d, n) * feats, feats), feats)
-
-    out_ref[:, columns(0)] = summed[0]
-
-    @pl.loop(1, n)
-    def _(s):
-        d = offset(s)
-        finish(d).wait_recv()
-        out_ref[:, columns(d)] = landed[d]
+            when_valid(s - 1, reduce_block)
+
+    when_valid(2 * n - 2, reduce_block)
+
+    def columns(z):
+        return pl.ds(pl.multiple_of(z * feats, feats), feats)
+
+    out_ref[:, columns(me)] = summed[me]
 
     @pl.loop(1, n)
     def _(d):
-        gather(d).wait_send()
-        finish(d).wait_send()
+        z = lax.rem(me + d, n)
+        finish(z, z).wait_recv()
+        out_ref[:, columns(z)] = landed[z]
+
+    @pl.loop(1, n)
+    def _(d):
+        z = lax.rem(me + d, n)
+        finish(z, z).wait_send()
 
     @pl.loop(0, n)
-    def _(d):
+    def _(k):
+        @pl.when(jnp.logical_and(k <= me, me + 1 < n))
+        def _():
+            hop(k, 1).wait_send()
+
+        @pl.when(jnp.logical_and(k >= me, me > 0))
+        def _():
+            hop(k, 0).wait_send()
+
         @pl.loop(1, peers)
         def _(e):
-            slab(d, e).wait_send()
+            slab(k, e).wait_send()
 
 
 def project(scaled, weight):
@@ -355,7 +360,7 @@
             pltpu.VMEM((n, own_rows, feats), jnp.bfloat16),
             pltpu.VMEM((n, own_rows, feats), jnp.bfloat16),
             dma((2,)),
-            dma((n,)),
+            dma((2, n)),
             dma((n,)),
             dma((n, peers)),
             dma((n, peers)),
@@ -401,9 +406,9 @@
         tok_rows, chan_width
     )
     to_end = jnp.exp(cumul[-1][None, :] - cumul)
-    x_end = (weighted * to_end[:, :, None]).reshape(tok_rows, chan_width).astype(jnp.bfloat16)
+    x_end = (weighted * to_end[:, :, None]).reshape(tok_rows, chan_width)
     total = jnp.repeat(cumul[-1], P_SIZE)[None, :]
-    y_off = earlier_blocks(x_end, b_group, total, c_group) * jnp.repeat(
+    y_off = carry(x_end, b_group, total, c_group) * jnp.repeat(
         jnp.exp(cumul), P_SIZE, axis=1
     )
     y_ssm = y_diag + y_off + (x_heads * skip[None, :, None]).reshape(tok_rows, chan_width)

time: 169 us -> 139 us (0.82)
  Pallas kernels: 120 us -> 91.6 us
    pallas_call x1, Pallas kernels: 43.8 us -> 27.9 us  [carry(): pl.pallas_call(functools.partial(carry_kernel, n, tile), out_shape=jax.Sh...]
    pallas_call x1, Pallas kernels: 73.6 us -> 61 us  [project(): pl.pallas_call(functools.partial(project_kernel, n, n_chan, n_sub, min(25...]
    unnamed x27 -> x26, local copies, waits for them, and re-layouts: 5.15 us -> 5.14 us
where the time goes in v1:
time: 139 us; the launch traced here: 138 us
  Pallas kernels  91.6 us (66%)
  local copies, waits for them, and re-layouts  19.8 us (14%)
  waiting for transfers between devices  12.3 us (9%)
  matrix products  6.65 us (5%)
  other arithmetic  5.95 us (4%)
  starting transfers between devices  1.63 us (1%)
    pallas_call x1, Pallas kernels, project(): pl.pallas_call(functools.partial(project_kernel, n, n_chan, n_sub, min(25...  61 us
    pallas_call x1, Pallas kernels, carry(): pl.pallas_call(functools.partial(carry_kernel, n, tile), out_shape=jax.Sh...  27.9 us
    ppermute x2, waiting for transfers between devices, partner_2(): return lax.ppermute(block, axis, route)  12.3 us
    dot_general x1, matrix products, body(): jnp.einsum('tuh,uhp->thp', mixing, weighted, precision=highest)  6.51 us
    unnamed x26, local copies, waits for them, and re-layouts  5.14 us
  transfers between devices with their start and end apart: 2, of which 2 were waited for; matrix products, arithmetic and copies ran while one was open for 1% of the time, Pallas kernels for 0%

profile of v1, /device:TPU:0, one launch (start us, length us, event | category | flops | bytes accessed | tf_op | source)
XLA Modules:
  0.0 138.2 jit_solution(13615815917313508737)
XLA Ops:
  0.0 0.8 copy.45
  0.8 0.2 reduce_window_sum.11
  1.1 1.2 constant_dynamic-slice_fusion
  2.7 0.3 copy.52
  3.1 1.1 mul.186
  4.1 1.6 %copy.50 = f32[128,2048]{1,0:T(8,128)S(1)} copy(f32[128,2048]{0,1:T(8,128)} %bitcast.29) | data formatting | bytes 2097152 | tf_op jit(solution)/shard_map/mul | solution.py:398
  5.8 1.2 copy.44
  7.2 6.5 %fusion = f32[32,64,128]{2,1,0:T(8,128)} fusion(f32[128,128]{1,0:T(8,128)S(1)} %fusion.25, f32[128,32]{0,1:T(8,128)S(1)} %copy.46, f32[128,32,64]{0,2,1:T(8,128)} %bitcast.30, pred[128,128]{1,0:T(8,128)(4,1)S(1)} %iota_compare_fusion, f32[128,32]{0,1:T(8,128)S(1)} %copy-done.6), kind=kOutput, calls=%fused_computation | convolution fusion | flops 405012480 | bytes 2211840 | tf_op jit(solution)/shard_map/tuh,uhp->thp/dot_general | solution.py:405
  13.7 2.5 %copy.55 = f32[128,2048]{1,0:T(8,128)} copy(f32[128,2048]{0,1:T(8,128)} %bitcast.31) | data formatting | bytes 2097152 | tf_op jit(solution)/shard_map/reshape | solution.py:405
  16.3 1.1 broadcast_in_dim.103
  17.3 2.6 %copy.54 = f32[128,2048]{1,0:T(8,128)} copy(f32[128,2048]{0,1:T(8,128)} %bitcast.27) | data formatting | bytes 2097152 | tf_op jit(solution)/shard_map/reshape | solution.py:411
  20.1 0.2 multiply_multiply_fusion.x_ref
  20.2 27.9 %shard_map.109 = f32[128,2048]{1,0:T(8,128)S(1)} custom-call(f32[128,2048]{1,0:T(8,128)S(1)} %multiply_multiply_fusion.x_ref, bf16[256,128]{1,0:T(8,128)(2,1)S(1)} %bitcast.24, f32[1,2048]{1,0:T(1,128)S(1)} %broadcast_in_dim_reshape.3.total_ref, bf16[128,256]{1,0:T(8,128)(2,1)S(1)} %bitcast.23), custom_call_target="tpu_custom_call" | custom-call | tf_op jit(solution)/shard_map/pallas_call | solution.py:124
  48.2 1.5 %fusion.41 = (f32[128,2048]{1,0:T(8,128)}, f32[128,2048]{1,0:T(8,128)S(1)}) fusion(bf16[128,2048]{1,0:T(8,128)(2,1)S(1)} %copy-done.5, f32[2048]{0:T(1024)S(1)} %mul.198, bf16[128,2048]{1,0:T(8,128)(2,1)S(1)} %copy-done.2, f32[128,2048]{1,0:T(8,128)S(1)} %copy-done.3, f32[128,2048]{1,0:T(8,128)S(1)} %shard_map.109, f32[128,2048]{1,0:T(8,128)S(1)} %copy-done.4), kind=kLoop, calls=%fused_computation.105 | loop fusion | flops 3145728 | bytes 6299648 | tf_op jit(solution)/shard_map/mul | solution.py:417
  49.7 2.1 %mul.204 = f32[128,2,1024]{2,1,0:T(2,128)S(1)} reshape(f32[128,2048]{1,0:T(8,128)} %get-tuple-element.11) | data formatting | bytes 2097152 | tf_op jit(solution)/shard_map/mul | solution.py:417
  51.8 0.3 reduce_sum.9
  52.2 0.3 mul.205
  52.5 0.3 copy.59
  52.9 0.2 fusion.19
  53.2 0.6 fusion.32
  53.8 1.2 collective-permute-done
  55.1 0.2 fusion.18
  55.3 1.6 %collective-permute-start.1 = (bf16[128,2048]{1,0:T(8,128)(2,1)S(1)}, bf16[128,2048]{1,0:T(8,128)(2,1)S(1)}, u32[]{:S(2)}, u32[]{:S(2)}) collective-permute-start(bf16[128,2048]{1,0:T(8,128)(2,1)S(1)} %fusion.18), channel_id=1, source_target_pairs={{0,2},{2,0},{1,3},{3,1},{4,6},{6,4},{5,7},{7,5},{8,10},{10,8},{9,1... | collective-permute-start | bytes 1572872 | tf_op jit(solution)/shard_map/ppermute | solution.py:31
  56.8 0.6 fusion.29
  57.4 0.8 fusion.24.table_ref
  58.2 11.1 %collective-permute-done.1 = bf16[128,2048]{1,0:T(8,128)(2,1)S(1)} collective-permute-done((bf16[128,2048]{1,0:T(8,128)(2,1)S(1)}, bf16[128,2048]{1,0:T(8,128)(2,1)S(1)}, u32[]{:S(2)}, u32[]{:S(2)}) %collective-permute-start.1) | collective-permute-done | bytes 524320 | tf_op jit(solution)/shard_map/ppermute | solution.py:31
  69.3 1.3 fusion.11.mixed_ref
  70.6 2.7 %shard_map.110.scaled_ref = bf16[128,2048]{1,0:T(8,128)(2,1)} custom-call(f32[128,2048]{1,0:T(8,128)} %fusion.11.mixed_ref, bf16[128,128]{1,0:T(8,128)(2,1)} %fusion.24.table_ref, f32[1,2048]{1,0:T(1,128)} %bitcast.33, f32[1,2048]{1,0:T(1,128)} %bitcast.32), custom_call_target="tpu_custom_call" | custom-call | tf_op jit(solution)/shard_map/pallas_call | solution.py:162
  73.3 2.2 %copy-done = bf16[2048,1024]{1,0:T(8,128)(2,1)S(1)} copy-done((bf16[2048,1024]{1,0:T(8,128)(2,1)S(1)}, bf16[2048,1024]{1,0:T(8,128)(2,1)}, u32[]{:S(2)}) %copy-start) | copy-done | bytes 4194328
  75.5 1.0 copy-done.1
  76.5 61.0 %shard_map.111 = bf16[32,4096]{1,0:T(8,128)(2,1)S(1)} custom-call(bf16[128,2048]{1,0:T(8,128)(2,1)S(1)} %copy-done.1, bf16[2048,1024]{1,0:T(8,128)(2,1)S(1)} %copy-done), custom_call_target="tpu_custom_call" | custom-call | tf_op jit(solution)/shard_map/pallas_call | solution.py:350
  137.5 0.7 copy.64
  (41 shorter events, 1.1 us)
Async XLA Ops:
  1.1 1.9 %copy-start.6 = (f32[128,32]{0,1:T(8,128)S(1)}, f32[128,32]{0,1:T(8,128)}, u32[]{:S(2)}) copy-start(f32[128,32]{0,1:T(8,128)} %param.14) | copy-start | bytes 49156
  3.1 2.8 %copy-start.2 = (bf16[128,2048]{1,0:T(8,128)(2,1)S(1)}, bf16[128,2048]{1,0:T(8,128)(2,1)}, u32[]{:S(2)}) copy-start(bf16[128,2048]{1,0:T(8,128)(2,1)} %param.11) | copy-start | bytes 1572868
  16.2 3.7 %copy-start.10 = (f32[32]{0:T(128)S(1)}, f32[32]{0:T(128)}, u32[]{:S(2)}) copy-start(f32[32]{0:T(128)} %param.16) | copy-start | bytes 388
  20.1 28.1 %copy-start.3 = (f32[128,2048]{1,0:T(8,128)S(1)}, f32[128,2048]{1,0:T(8,128)}, u32[]{:S(2)}) copy-start(f32[128,2048]{1,0:T(8,128)} %copy.55) | copy-start | bytes 3145732
  20.1 28.1 %copy-start.4 = (f32[128,2048]{1,0:T(8,128)S(1)}, f32[128,2048]{1,0:T(8,128)}, u32[]{:S(2)}) copy-start(f32[128,2048]{1,0:T(8,128)} %copy.54) | copy-start | bytes 3145732
  20.1 28.1 %copy-start.5 = (bf16[128,2048]{1,0:T(8,128)(2,1)S(1)}, bf16[128,2048]{1,0:T(8,128)(2,1)}, u32[]{:S(2)}) copy-start(bf16[128,2048]{1,0:T(8,128)(2,1)} %param.17) | copy-start | bytes 1572868
  51.8 1.1 copy-start.8
  51.8 1.1 copy-start.7
  52.5 0.7 copy-start.9
  53.1 2.0 %collective-permute-start = (bf16[128,2048]{1,0:T(8,128)(2,1)S(1)}, bf16[128,2048]{1,0:T(8,128)(2,1)S(1)}, u32[]{:S(2)}, u32[]{:S(2)}) collective-permute-start(bf16[128,2048]{1,0:T(8,128)(2,1)S(1)} %fusion.19), channel_id=1, source_target_pairs={{0,1},{1,0},{2,3},{3,2},{4,5},{5,4},{6,7},{7,6},{8,9},{9,8},{10,11... | collective-permute-start | bytes 1572872 | tf_op jit(solution)/shard_map/ppermute | solution.py:31
  55.3 14.0 %collective-permute-start.1 = (bf16[128,2048]{1,0:T(8,128)(2,1)S(1)}, bf16[128,2048]{1,0:T(8,128)(2,1)S(1)}, u32[]{:S(2)}, u32[]{:S(2)}) collective-permute-start(bf16[128,2048]{1,0:T(8,128)(2,1)S(1)} %fusion.18), channel_id=1, source_target_pairs={{0,2},{2,0},{1,3},{3,1},{4,6},{6,4},{5,7},{7,5},{8,10},{10,8},{9,1... | collective-permute-start | bytes 1572872 | tf_op jit(solution)/shard_map/ppermute | solution.py:31
  73.3 2.2 %copy-start = (bf16[2048,1024]{1,0:T(8,128)(2,1)S(1)}, bf16[2048,1024]{1,0:T(8,128)(2,1)}, u32[]{:S(2)}) copy-start(bf16[2048,1024]{1,0:T(8,128)(2,1)} %weight_hbm.1) | copy-start | bytes 12582916
  75.5 1.0 copy-start.1

commit v2 on v1

--- a/solution.py
+++ b/solution.py
@@ -60,15 +60,60 @@
     return jnp.dot(left, right, preferred_element_type=jnp.float32)
 
 
-def carry_kernel(
-    n, tile, x_ref, bt_ref, total_ref, c_ref, y_ref, arrived, leaving, send, recv
+def mixer_kernel(
+    n,
+    tile,
+    x_ref,
+    bt_ref,
+    c_ref,
+    cum_ref,
+    step_ref,
+    cumt_ref,
+    stept_ref,
+    skip_ref,
+    y_ref,
+    arrived,
+    leaving,
+    inner_ref,
+    send,
+    recv,
 ):
     me = lax.axis_index("seq")
     right, left = lax.rem(me + 1, n), lax.rem(me + n - 1, n)
     barrier = pltpu.get_barrier_semaphore()
     for near in (left, right):
         pl.semaphore_signal(barrier, inc=1, device_id={"seq": near}, device_id_type=MESH)
-    pl.semaphore_wait(barrier, 2)
+
+    rows, width = y_ref.shape
+    tiles = width // tile
+    cum = cum_ref[...]
+    total = cum_ref[rows - 1 : rows, :]
+    to_end = step_ref[...] * jnp.exp(total - cum)
+    since = jnp.exp(cum)
+    whole = jnp.exp(total)
+    causal = lax.broadcasted_iota(jnp.int32, (rows, rows), 0) >= lax.broadcasted_iota(
+        jnp.int32, (rows, rows), 1
+    )
+    inner_ref[...] = jnp.where(causal, dot32(c_ref[...], bt_ref[...]), 0.0)
+
+    def pick(first, second):
+        shape = (max(first.shape[0], second.shape[0]), lanes)
+        low = lax.broadcasted_iota(jnp.int32, shape, 1) < P_SIZE
+        return jnp.where(low, first, second)
+
+    def spread(values, i):
+        pairs = range(i * tile // P_SIZE, (i + 1) * tile // P_SIZE, lanes // P_SIZE)
+        return jnp.concatenate(
+            [pick(values[:, h : h + 1], values[:, h + 1 : h + 2]) for h in pairs], axis=1
+        )
+
+    def diagonal(h, block):
+        differ = cum[:, h : h + 1] - cumt_ref[h : h + 1, :]
+        mixing = jnp.exp(jnp.minimum(differ, 0.0)) * inner_ref[...] * stept_ref[h : h + 1, :]
+        upper, lower = halves(mixing)
+        return dot32(
+            jnp.concatenate([upper, lower], axis=1), jnp.concatenate([block, block], axis=0)
+        )
 
     def copy(i):
         return pltpu.make_async_remote_copy(
@@ -80,22 +125,22 @@
             device_id_type=MESH,
         )
 
-    @pl.loop(0, y_ref.shape[1] // tile)
-    def _(i):
-        at = pl.ds(pl.multiple_of(i * tile, tile), tile)
-        upper, lower = halves(x_ref[:, at])
+    pl.semaphore_wait(barrier, 2)
+
+    for i in range(tiles):
+        at = slice(i * tile, (i + 1) * tile)
+        x_tile = x_ref[:, at].astype(jnp.float32)
+        upper, lower = halves(x_tile * spread(to_end, i))
         own = dot32(bt_ref[...], upper) + dot32(bt_ref[...], lower)
 
         @pl.when(me == 0)
         def _():
             leaving[i] = own.astype(jnp.bfloat16)
-            y_ref[:, at] = jnp.zeros((y_ref.shape[0], tile), jnp.float32)
 
         @pl.when(me > 0)
         def _():
             copy(i).wait_recv()
-            state = arrived[i]
-            leaving[i] = (state.astype(jnp.float32) * jnp.exp(total_ref[:, at]) + own).astype(
+            leaving[i] = (arrived[i].astype(jnp.float32) * spread(whole, i) + own).astype(
                 jnp.bfloat16
             )
 
@@ -103,39 +148,57 @@
         def _():
             copy(i).start()
 
+        for k in range(i * tile, (i + 1) * tile, lanes):
+            here = slice(k, k + lanes)
+            block = x_ref[:, here]
+            h = k // P_SIZE
+            y_ref[:, here] = (
+                pick(diagonal(h, block), diagonal(h + 1, block))
+                + block.astype(jnp.float32) * skip_ref[:, here]
+            )
+
         @pl.when(me > 0)
         def _():
-            y_ref[:, at] = dot32(c_ref[...], arrived[i])
+            y_ref[:, at] += dot32(c_ref[...], arrived[i]) * spread(since, i)
 
     @pl.when(me + 1 < n)
     def _():
-        @pl.loop(0, y_ref.shape[1] // tile)
-        def _(i):
+        for i in range(tiles):
             copy(i).wait_send()
 
 
-def carry(x_end, b_group, total, c_group):
+def mixer(x_in, b_group, c_group, cumul, step_size, skip):
     n = lax.axis_size("seq")
-    rows, width = x_end.shape
+    rows, width = x_in.shape
     tile = min(256, width)
     tiles = width // tile
     states = b_group.shape[1]
     vmem = pl.BlockSpec(memory_space=pltpu.VMEM)
     return pl.pallas_call(
-        functools.partial(carry_kernel, n, tile),
+        functools.partial(mixer_kernel, n, tile),
         out_shape=jax.ShapeDtypeStruct((rows, width), jnp.float32),
-        in_specs=[vmem] * 4,
+        in_specs=[vmem] * 8,
         out_specs=vmem,
         scratch_shapes=[
             pltpu.VMEM((tiles, states, tile), jnp.bfloat16),
             pltpu.VMEM((tiles, states, tile), jnp.bfloat16),
+            pltpu.VMEM((rows, rows), jnp.float32),
             pltpu.SemaphoreType.DMA((tiles,)),
             pltpu.SemaphoreType.DMA((tiles,)),
         ],
         compiler_params=pltpu.CompilerParams(
             collective_id=0, has_side_effects=True, vmem_limit_bytes=48 * 2**20
         ),
-    )(x_end, b_group.T, total, c_group)
+    )(
+        x_in,
+        b_group.T,
+        c_group,
+        cumul,
+        step_size,
+        cumul.T,
+        step_size.T,
+        jnp.repeat(skip, P_SIZE)[None, :],
+    )
 
 
 def rotate_kernel(factor, mixed_ref, table_ref, up_ref, down_ref, out_ref):
@@ -368,7 +431,7 @@
             dma((n,)),
         ],
         compiler_params=pltpu.CompilerParams(
-            collective_id=1, has_side_effects=True, vmem_limit_bytes=48 * 2**20
+            collective_id=1, has_side_effects=True, vmem_limit_bytes=60 * 2**20
         ),
     )(scaled, weight)
 
@@ -386,7 +449,6 @@
     channel_shift_power,
     out_weight,
 ):
-    highest = lax.Precision.HIGHEST
     tok_rows, chan_width = x_in.shape
     head_local = step_size.shape[1]
     head_group = LOCAL_HEADS // G
@@ -394,24 +456,7 @@
     group_local = sub_index * head_local // head_group
     b_group = lax.dynamic_slice_in_dim(b_in, group_local, 1, 1)[:, 0, :]
     c_group = lax.dynamic_slice_in_dim(c_in, group_local, 1, 1)[:, 0, :]
-    x_heads = x_in.astype(jnp.float32).reshape(tok_rows, head_local, P_SIZE)
-    weighted = x_heads * step_size[:, :, None]
-    cumul = jnp.cumsum(log_decay, axis=0)
-    inner = jnp.dot(c_group, b_group.T, preferred_element_type=jnp.float32)
-    differ = cumul[:, None, :] - cumul[None, :, :]
-    causal = (jnp.arange(tok_rows)[:, None] >= jnp.arange(tok_rows)[None, :])[:, :, None]
-    ratio = jnp.where(causal, jnp.exp(jnp.where(causal, differ, 0.0)), 0.0)
-    mixing = ratio * inner[:, :, None]
-    y_diag = jnp.einsum("tuh,uhp->thp", mixing, weighted, precision=highest).reshape(
-        tok_rows, chan_width
-    )
-    to_end = jnp.exp(cumul[-1][None, :] - cumul)
-    x_end = (weighted * to_end[:, :, None]).reshape(tok_rows, chan_width)
-    total = jnp.repeat(cumul[-1], P_SIZE)[None, :]
-    y_off = carry(x_end, b_group, total, c_group) * jnp.repeat(
-        jnp.exp(cumul), P_SIZE, axis=1
-    )
-    y_ssm = y_diag + y_off + (x_heads * skip[None, :, None]).reshape(tok_rows, chan_width)
+    y_ssm = mixer(x_in, b_group, c_group, jnp.cumsum(log_decay, axis=0), step_size, skip)
     gated_pre = y_ssm * jax.nn.silu(gate_in.astype(jnp.float32))
     grouped = gated_pre.reshape(tok_rows, head_local // NORM_HEADS, NORM_HEADS * P_SIZE)
     mean_sq = jnp.mean(grouped * grouped, axis=2, keepdims=True)

time: 139 us -> 123 us (0.88)
  local copies, waits for them, and re-layouts: 19.8 us -> 8.92 us
  matrix products: 6.65 us -> 0 us
  Pallas kernels: 91.6 us -> 93.8 us
    dot_general x2 -> x0, matrix products: 6.65 us -> none  [the longest x1 6.51 us: body(): jnp.einsum('tuh,uhp->thp', mixing, weighted, precision=highest)]
    reshape x2 -> x0, local copies, waits for them, and re-layouts: 5.1 us -> none  [the longest x1 2.56 us: body(): jnp.repeat(jnp.exp(cumul), P_SIZE, axis=1)]
    mul x6 -> x0, local copies, waits for them, and re-layouts: 3.16 us -> none  [the longest x2 2.6 us: body(): weighted = x_heads * step_size[:, :, None]]
    pallas_call x1, Pallas kernels: 61 us -> 63 us  [project(): pl.pallas_call(functools.partial(project_kernel, n, n_chan, n_sub, min(25...]
    unnamed x26 -> x17, local copies, waits for them, and re-layouts: 5.14 us -> 5.46 us
  transfers between devices with their start and end apart: 2 -> 2, of which waited for: 2 -> 2; matrix products, arithmetic and copies ran while one was open for 1% -> 2% of each run, Pallas kernels for 0% -> 0%
where the time goes in v2:
time: 123 us
  Pallas kernels  93.8 us (76%)
  waiting for transfers between devices  12.3 us (10%)
  local copies, waits for them, and re-layouts  8.92 us (7%)
  other arithmetic  5.81 us (5%)
  starting transfers between devices  1.63 us (1%)
    pallas_call x1, Pallas kernels, project(): pl.pallas_call(functools.partial(project_kernel, n, n_chan, n_sub, min(25...  63 us
    pallas_call x1, Pallas kernels, mixer(): pl.pallas_call(functools.partial(mixer_kernel, n, tile), out_shape=jax.Sh...  28.1 us
    ppermute x2, waiting for transfers between devices, partner_2(): return lax.ppermute(block, axis, route)  12.3 us
    unnamed x17, local copies, waits for them, and re-layouts  5.46 us
    pallas_call x1, Pallas kernels, rotate(): pl.pallas_call(functools.partial(rotate_kernel, 1.0 / math.sqrt(LOCAL_HEA...  2.69 us
  transfers between devices with their start and end apart: 2, of which 2 were waited for; matrix products, arithmetic and copies ran while one was open for 2% of the time, Pallas kernels for 0%

profile of v2, /device:TPU:0, one launch (start us, length us, event | category | flops | bytes accessed | tf_op | source)
XLA Modules:
  0.0 122.6 jit_solution(8398558502664238069)
XLA Ops:
  0.0 1.2 %constant_dynamic-slice_fusion = (bf16[128,1,256]{2,1,0:T(2,128)(2,1)S(1)}, bf16[128,1,256]{2,1,0:T(2,128)(2,1)S(1)}) fusion(bf16[128,2,256]{2,1,0:T(2,128)(2,1)} %param.13, s32[]{:T(128)S(6)} %select_n.288, bf16[128,2,256]{2,1,0:T(2,128)(2,1)} %param.12), kind=kLoop, calls=%fused_computation.83 | loop fusion | bytes 262148 | tf_op jit(solution)/shard_map/dynamic_slice | solution.py:458
  1.2 0.1 copy.27
  1.4 0.8 copy.29
  2.2 0.2 reduce_window_sum.11.cum_ref
  2.4 0.1 copy.30
  2.4 0.8 copy.31.step_ref
  3.3 0.7 broadcast_in_dim.70
  4.0 0.1 broadcast_in_dim_reshape.3.skip_ref
  4.1 1.0 copy-done
  5.1 0.7 copy-done.1
  5.9 28.1 %shard_map.109 = f32[128,2048]{1,0:T(8,128)S(1)} custom-call(bf16[128,2048]{1,0:T(8,128)(2,1)S(1)} %copy-done, bf16[256,128]{1,0:T(8,128)(2,1)S(1)} %bitcast.12, bf16[128,256]{1,0:T(8,128)(2,1)S(1)} %bitcast.13, f32[128,32]{1,0:T(8,128)S(1)} %reduce_window_sum.11.cum_ref, f32[128,32]{1,0:T(8,128)S(1)} %copy.31.step_ref, f32[32,128]{1,0:T(8,128)S(1)} %bitcast.15, ...), custom_call_target="tpu_custom_call" | custom-call | tf_op jit(solution)/shard_map/pallas_call | solution.py:177
  33.9 0.0 copy-start.4
  34.0 0.0 copy-start.3
  34.0 1.3 %fusion.25 = f32[128,2048]{1,0:T(8,128)S(1)} fusion(f32[128,2048]{1,0:T(8,128)S(1)} %shard_map.109, bf16[128,2048]{1,0:T(8,128)(2,1)} %param.17), kind=kLoop, calls=%fused_computation.85 | loop fusion | flops 1835008 | bytes 2621440 | tf_op jit(solution)/shard_map/mul | solution.py:462
  35.3 0.9 mul.142
  36.2 0.0 copy-start.5
  36.2 0.3 reduce_sum.9
  36.6 0.3 mul.143
  37.0 0.3 copy.35
  37.3 0.4 fusion.7
  37.8 0.1 collective-permute-start
  37.9 0.6 fusion.17
  38.5 1.2 collective-permute-done
  39.7 0.2 fusion.6
  39.9 1.6 %collective-permute-start.1 = (bf16[128,2048]{1,0:T(8,128)(2,1)S(1)}, bf16[128,2048]{1,0:T(8,128)(2,1)S(1)}, u32[]{:S(2)}, u32[]{:S(2)}) collective-permute-start(bf16[128,2048]{1,0:T(8,128)(2,1)S(1)} %fusion.6), channel_id=1, source_target_pairs={{0,2},{2,0},{1,3},{3,1},{4,6},{6,4},{5,7},{7,5},{8,10},{10,8},{9,1... | collective-permute-start | bytes 1572872 | tf_op jit(solution)/shard_map/ppermute | solution.py:31
  41.5 0.6 fusion.14
  42.1 0.8 fusion.11.table_ref
  42.9 11.0 %collective-permute-done.1 = bf16[128,2048]{1,0:T(8,128)(2,1)S(1)} collective-permute-done((bf16[128,2048]{1,0:T(8,128)(2,1)S(1)}, bf16[128,2048]{1,0:T(8,128)(2,1)S(1)}, u32[]{:S(2)}, u32[]{:S(2)}) %collective-permute-start.1) | collective-permute-done | bytes 524320 | tf_op jit(solution)/shard_map/ppermute | solution.py:31
  54.0 1.3 %fusion.5.mixed_ref = f32[128,2048]{1,0:T(8,128)} fusion(bf16[128,2048]{1,0:T(8,128)(2,1)S(1)} %collective-permute-done.1, bf16[128,2048]{1,0:T(8,128)(2,1)S(1)} %fusion.7, bf16[128,2048]{1,0:T(8,128)(2,1)S(1)} %collective-permute-done, pred[]{:T(512)S(6)} %eq.51, pred[]{:T(512)S(6)} %eq.50), kind=kLoop, calls=%fused_computation.11 | loop fusion | flops 2359296 | bytes 2621442 | tf_op jit(solution)/shard_map/jit(_where)/select_n | solution.py:476
  55.2 2.7 %shard_map.110.scaled_ref = bf16[128,2048]{1,0:T(8,128)(2,1)} custom-call(f32[128,2048]{1,0:T(8,128)} %fusion.5.mixed_ref, bf16[128,128]{1,0:T(8,128)(2,1)} %fusion.11.table_ref, f32[1,2048]{1,0:T(1,128)} %bitcast.19, f32[1,2048]{1,0:T(1,128)} %bitcast.18), custom_call_target="tpu_custom_call" | custom-call | tf_op jit(solution)/shard_map/pallas_call | solution.py:225
  57.9 63.0 %shard_map.111 = bf16[32,4096]{1,0:T(8,128)(2,1)} custom-call(bf16[128,2048]{1,0:T(8,128)(2,1)} %shard_map.110.scaled_ref, bf16[2048,1024]{1,0:T(8,128)(2,1)} %weight_hbm.1), custom_call_target="tpu_custom_call" | custom-call | tf_op jit(solution)/shard_map/pallas_call | solution.py:413
  120.9 1.7 %copy.40 = bf16[32,4096]{1,0:T(8,128)(2,1)} copy(bf16[32,4096]{1,0:T(8,128)(2,1)} %shard_map.111) | data formatting | bytes 524288
  (14 shorter events, 0.1 us)
Async XLA Ops:
  4.1 1.0 copy-start
  5.1 0.7 copy-start.1
  33.9 3.4 %copy-start.4 = (s32[2048]{0:T(1024)S(1)}, s32[2048]{0:T(1024)}, u32[]{:S(2)}) copy-start(s32[2048]{0:T(1024)} %param.19) | copy-start | bytes 24580
  34.0 3.4 %copy-start.3 = (f32[2048]{0:T(1024)S(1)}, f32[2048]{0:T(1024)}, u32[]{:S(2)}) copy-start(f32[2048]{0:T(1024)} %param.18) | copy-start | bytes 24580
  36.2 1.1 copy-start.2
  36.2 1.7 %copy-start.5 = (s32[2048]{0:T(1024)S(1)}, s32[2048]{0:T(1024)}, u32[]{:S(2)}) copy-start(s32[2048]{0:T(1024)} %param.20) | copy-start | bytes 24580
  37.8 2.0 %collective-permute-start = (bf16[128,2048]{1,0:T(8,128)(2,1)S(1)}, bf16[128,2048]{1,0:T(8,128)(2,1)S(1)}, u32[]{:S(2)}, u32[]{:S(2)}) collective-permute-start(bf16[128,2048]{1,0:T(8,128)(2,1)S(1)} %fusion.7), channel_id=1, source_target_pairs={{0,1},{1,0},{2,3},{3,2},{4,5},{5,4},{6,7},{7,6},{8,9},{9,8},{10,11... | collective-permute-start | bytes 1572872 | tf_op jit(solution)/shard_map/ppermute | solution.py:31
  39.9 14.0 %collective-permute-start.1 = (bf16[128,2048]{1,0:T(8,128)(2,1)S(1)}, bf16[128,2048]{1,0:T(8,128)(2,1)S(1)}, u32[]{:S(2)}, u32[]{:S(2)}) collective-permute-start(bf16[128,2048]{1,0:T(8,128)(2,1)S(1)} %fusion.6), channel_id=1, source_target_pairs={{0,2},{2,0},{1,3},{3,1},{4,6},{6,4},{5,7},{7,5},{8,10},{10,8},{9,1... | collective-permute-start | bytes 1572872 | tf_op jit(solution)/shard_map/ppermute | solution.py:31

commit v3 on v2

--- a/solution.py
+++ b/solution.py
@@ -18,6 +18,7 @@
 clip_level = 4.0
 expo_levels = (-1, 0, 1, 2, 3)
 lanes = 128
+pieces = 2
 MESH = pl.DeviceIdType.MESH
 
 
@@ -279,15 +280,14 @@
 
     pl.semaphore_wait(barrier, n - 1 + peers - 1)
 
-    def block_at(s):
-        return me + jnp.where(lax.rem(s, 2) == 1, -((s + 1) // 2), s // 2)
-
-    def hop(k, way):
+    piece = slots.shape[1] // pieces
+
+    def hop(k, q, way):
         return pltpu.make_async_remote_copy(
-            src_ref=slots.at[k],
-            dst_ref=slots.at[k],
-            send_sem=g_send.at[way, k],
-            recv_sem=g_recv.at[k],
+            src_ref=slots.at[k, pl.ds(q * piece, piece)],
+            dst_ref=slots.at[k, pl.ds(q * piece, piece)],
+            send_sem=g_send.at[way, k, q],
+            recv_sem=g_recv.at[k, q],
             device_id={"seq": lax.rem(me + (1 if way == 1 else n - 1), n)},
             device_id_type=MESH,
         )
@@ -313,30 +313,26 @@
             device_id_type=MESH,
         )
 
-    def when_valid(s, act):
-        k = block_at(s)
+    def when_valid(k, act):
         pl.when(jnp.logical_and(k >= 0, k < n))(lambda: act(k))
 
+    def to_right(k, q):
+        @pl.when(me + 1 < n)
+        def _():
+            hop(k, q, 1).start()
+
+    def to_left(k, q):
+        @pl.when(me > 0)
+        def _():
+            hop(k, q, 0).start()
+
     own.wait()
-
-    def pass_on(k):
-        @pl.when(jnp.logical_and(k <= me, me + 1 < n))
-        def _():
-            hop(k, 1).start()
-
-        @pl.when(jnp.logical_and(k >= me, me > 0))
-        def _():
-            hop(k, 0).start()
-
-    pass_on(me)
+    for q in range(pieces):
+        to_right(me, q)
+        to_left(me, q)
     fetch.wait()
 
     def project_block(k):
-        @pl.when(k != me)
-        def _():
-            hop(k, 1).wait_recv()
-            pass_on(k)
-
         @pl.loop(0, feats // tile)
         def _(i):
             at = pl.ds(pl.multiple_of(i * tile, tile), tile)
@@ -361,15 +357,37 @@
         def _():
             finish(k, me).start()
 
-    @pl.loop(0, 2 * n - 1)
-    def _(s):
-        when_valid(s, project_block)
-
-        @pl.when(s > 0)
-        def _():
-            when_valid(s - 1, reduce_block)
-
-    when_valid(2 * n - 2, reduce_block)
+    project_block(me)
+
+    @pl.loop(1, n)
+    def _(j):
+        for q in range(pieces):
+
+            def from_left(k, q=q):
+                hop(k, q, 1).wait_recv()
+                to_right(k, q)
+
+            def from_right(k, q=q):
+                hop(k, q, 0).wait_recv()
+                to_left(k, q)
+
+            when_valid(me - j, from_left)
+            when_valid(me + j, from_right)
+
+        when_valid(me - j, project_block)
+        when_valid(me + j, project_block)
+
+        @pl.when(j == 1)
+        def _():
+            reduce_block(me)
+
+        @pl.when(j > 1)
+        def _():
+            when_valid(me - j + 1, reduce_block)
+            when_valid(me + j - 1, reduce_block)
+
+    when_valid(me - n + 1, reduce_block)
+    when_valid(me + n - 1, reduce_block)
 
     def columns(z):
         return pl.ds(pl.multiple_of(z * feats, feats), feats)
@@ -391,11 +409,13 @@
     def _(k):
         @pl.when(jnp.logical_and(k <= me, me + 1 < n))
         def _():
-            hop(k, 1).wait_send()
+            for q in range(pieces):
+                hop(k, q, 1).wait_send()
 
         @pl.when(jnp.logical_and(k >= me, me > 0))
         def _():
-            hop(k, 0).wait_send()
+            for q in range(pieces):
+                hop(k, q, 0).wait_send()
 
         @pl.loop(1, peers)
         def _(e):
@@ -423,8 +443,8 @@
             pltpu.VMEM((n, own_rows, feats), jnp.bfloat16),
             pltpu.VMEM((n, own_rows, feats), jnp.bfloat16),
             dma((2,)),
-            dma((2, n)),
-            dma((n,)),
+            dma((2, n, pieces)),
+            dma((n, pieces)),
             dma((n, peers)),
             dma((n, peers)),
             dma((n,)),

time: 123 us -> 122 us (level)
  no operation moved by 1% of the time
where the time goes in v3:
time: 122 us
  Pallas kernels  92.9 us (76%)
  waiting for transfers between devices  12.3 us (10%)
  local copies, waits for them, and re-layouts  8.92 us (7%)
  other arithmetic  5.81 us (5%)
  starting transfers between devices  1.63 us (1%)
    pallas_call x1, Pallas kernels, project(): pl.pallas_call(functools.partial(project_kernel, n, n_chan, n_sub, min(25...  62.2 us
    pallas_call x1, Pallas kernels, mixer(): pl.pallas_call(functools.partial(mixer_kernel, n, tile), out_shape=jax.Sh...  28.1 us
    ppermute x2, waiting for transfers between devices, partner_2(): return lax.ppermute(block, axis, route)  12.3 us
    unnamed x17, local copies, waits for them, and re-layouts  5.46 us
    pallas_call x1, Pallas kernels, rotate(): pl.pallas_call(functools.partial(rotate_kernel, 1.0 / math.sqrt(LOCAL_HEA...  2.69 us
  transfers between devices with their start and end apart: 2, of which 2 were waited for; matrix products, arithmetic and copies ran while one was open for 2% of the time, Pallas kernels for 0%

profile of v3, /device:TPU:0, one launch (start us, length us, event | category | flops | bytes accessed | tf_op | source)
XLA Modules:
  0.0 121.8 jit_solution(6078665257590561051)
XLA Ops:
  0.0 1.2 %constant_dynamic-slice_fusion = (bf16[128,1,256]{2,1,0:T(2,128)(2,1)S(1)}, bf16[128,1,256]{2,1,0:T(2,128)(2,1)S(1)}) fusion(bf16[128,2,256]{2,1,0:T(2,128)(2,1)} %param.13, s32[]{:T(128)S(6)} %select_n.288, bf16[128,2,256]{2,1,0:T(2,128)(2,1)} %param.12), kind=kLoop, calls=%fused_computation.83 | loop fusion | bytes 262148 | tf_op jit(solution)/shard_map/dynamic_slice | solution.py:478
  1.2 0.1 copy.27
  1.4 0.8 copy.29
  2.2 0.2 reduce_window_sum.11.cum_ref
  2.4 0.1 copy.30
  2.4 0.8 copy.31.step_ref
  3.3 0.7 broadcast_in_dim.70
  4.0 0.1 broadcast_in_dim_reshape.3.skip_ref
  4.1 1.0 copy-done
  5.1 0.7 copy-done.1
  5.9 28.1 %shard_map.109 = f32[128,2048]{1,0:T(8,128)S(1)} custom-call(bf16[128,2048]{1,0:T(8,128)(2,1)S(1)} %copy-done, bf16[256,128]{1,0:T(8,128)(2,1)S(1)} %bitcast.12, bf16[128,256]{1,0:T(8,128)(2,1)S(1)} %bitcast.13, f32[128,32]{1,0:T(8,128)S(1)} %reduce_window_sum.11.cum_ref, f32[128,32]{1,0:T(8,128)S(1)} %copy.31.step_ref, f32[32,128]{1,0:T(8,128)S(1)} %bitcast.15, ...), custom_call_target="tpu_custom_call" | custom-call | tf_op jit(solution)/shard_map/pallas_call | solution.py:178
  33.9 0.0 copy-start.4
  34.0 0.0 copy-start.3
  34.0 1.3 %fusion.25 = f32[128,2048]{1,0:T(8,128)S(1)} fusion(f32[128,2048]{1,0:T(8,128)S(1)} %shard_map.109, bf16[128,2048]{1,0:T(8,128)(2,1)} %param.17), kind=kLoop, calls=%fused_computation.85 | loop fusion | flops 1835008 | bytes 2621440 | tf_op jit(solution)/shard_map/mul | solution.py:482
  35.3 0.9 mul.142
  36.2 0.0 copy-start.2
  36.2 0.3 reduce_sum.9
  36.6 0.3 mul.143
  37.0 0.3 copy.35
  37.3 0.4 fusion.7
  37.8 0.1 collective-permute-start
  37.9 0.6 fusion.17
  38.5 1.2 %collective-permute-done = bf16[128,2048]{1,0:T(8,128)(2,1)S(1)} collective-permute-done((bf16[128,2048]{1,0:T(8,128)(2,1)S(1)}, bf16[128,2048]{1,0:T(8,128)(2,1)S(1)}, u32[]{:S(2)}, u32[]{:S(2)}) %collective-permute-start) | collective-permute-done | bytes 524320 | tf_op jit(solution)/shard_map/ppermute | solution.py:32
  39.7 0.2 fusion.6
  39.9 1.6 %collective-permute-start.1 = (bf16[128,2048]{1,0:T(8,128)(2,1)S(1)}, bf16[128,2048]{1,0:T(8,128)(2,1)S(1)}, u32[]{:S(2)}, u32[]{:S(2)}) collective-permute-start(bf16[128,2048]{1,0:T(8,128)(2,1)S(1)} %fusion.6), channel_id=1, source_target_pairs={{0,2},{2,0},{1,3},{3,1},{4,6},{6,4},{5,7},{7,5},{8,10},{10,8},{9,1... | collective-permute-start | bytes 1572872 | tf_op jit(solution)/shard_map/ppermute | solution.py:32
  41.5 0.6 fusion.14
  42.1 0.8 fusion.11.table_ref
  42.9 11.0 %collective-permute-done.1 = bf16[128,2048]{1,0:T(8,128)(2,1)S(1)} collective-permute-done((bf16[128,2048]{1,0:T(8,128)(2,1)S(1)}, bf16[128,2048]{1,0:T(8,128)(2,1)S(1)}, u32[]{:S(2)}, u32[]{:S(2)}) %collective-permute-start.1) | collective-permute-done | bytes 524320 | tf_op jit(solution)/shard_map/ppermute | solution.py:32
  54.0 1.3 %fusion.5.mixed_ref = f32[128,2048]{1,0:T(8,128)} fusion(bf16[128,2048]{1,0:T(8,128)(2,1)S(1)} %collective-permute-done.1, bf16[128,2048]{1,0:T(8,128)(2,1)S(1)} %fusion.7, bf16[128,2048]{1,0:T(8,128)(2,1)S(1)} %collective-permute-done, pred[]{:T(512)S(6)} %eq.51, pred[]{:T(512)S(6)} %eq.50), kind=kLoop, calls=%fused_computation.11 | loop fusion | flops 2359296 | bytes 2621442 | tf_op jit(solution)/shard_map/jit(_where)/select_n | solution.py:496
  55.2 2.7 %shard_map.110.scaled_ref = bf16[128,2048]{1,0:T(8,128)(2,1)} custom-call(f32[128,2048]{1,0:T(8,128)} %fusion.5.mixed_ref, bf16[128,128]{1,0:T(8,128)(2,1)} %fusion.11.table_ref, f32[1,2048]{1,0:T(1,128)} %bitcast.19, f32[1,2048]{1,0:T(1,128)} %bitcast.18), custom_call_target="tpu_custom_call" | custom-call | tf_op jit(solution)/shard_map/pallas_call | solution.py:226
  57.9 62.2 %shard_map.111 = bf16[32,4096]{1,0:T(8,128)(2,1)} custom-call(bf16[128,2048]{1,0:T(8,128)(2,1)} %shard_map.110.scaled_ref, bf16[2048,1024]{1,0:T(8,128)(2,1)} %weight_hbm.1), custom_call_target="tpu_custom_call" | custom-call | tf_op jit(solution)/shard_map/pallas_call | solution.py:433
  120.1 1.7 %copy.40 = bf16[32,4096]{1,0:T(8,128)(2,1)} copy(bf16[32,4096]{1,0:T(8,128)(2,1)} %shard_map.111) | data formatting | bytes 524288
  (14 shorter events, 0.1 us)
Async XLA Ops:
  4.1 1.0 copy-start
  5.1 0.7 copy-start.1
  33.9 3.4 %copy-start.4 = (s32[2048]{0:T(1024)S(1)}, s32[2048]{0:T(1024)}, u32[]{:S(2)}) copy-start(s32[2048]{0:T(1024)} %param.19) | copy-start | bytes 24580
  34.0 3.4 %copy-start.3 = (f32[2048]{0:T(1024)S(1)}, f32[2048]{0:T(1024)}, u32[]{:S(2)}) copy-start(f32[2048]{0:T(1024)} %param.18) | copy-start | bytes 24580
  36.2 1.1 copy-start.2
  36.2 1.7 %copy-start.5 = (s32[2048]{0:T(1024)S(1)}, s32[2048]{0:T(1024)}, u32[]{:S(2)}) copy-start(s32[2048]{0:T(1024)} %param.20) | copy-start | bytes 24580
  37.8 2.0 %collective-permute-start = (bf16[128,2048]{1,0:T(8,128)(2,1)S(1)}, bf16[128,2048]{1,0:T(8,128)(2,1)S(1)}, u32[]{:S(2)}, u32[]{:S(2)}) collective-permute-start(bf16[128,2048]{1,0:T(8,128)(2,1)S(1)} %fusion.7), channel_id=1, source_target_pairs={{0,1},{1,0},{2,3},{3,2},{4,5},{5,4},{6,7},{7,6},{8,9},{9,8},{10,11... | collective-permute-start | bytes 1572872 | tf_op jit(solution)/shard_map/ppermute | solution.py:32
  39.9 14.0 %collective-permute-start.1 = (bf16[128,2048]{1,0:T(8,128)(2,1)S(1)}, bf16[128,2048]{1,0:T(8,128)(2,1)S(1)}, u32[]{:S(2)}, u32[]{:S(2)}) collective-permute-start(bf16[128,2048]{1,0:T(8,128)(2,1)S(1)} %fusion.6), channel_id=1, source_target_pairs={{0,2},{2,0},{1,3},{3,1},{4,6},{6,4},{5,7},{7,5},{8,10},{10,8},{9,1... | collective-permute-start | bytes 1572872 | tf_op jit(solution)/shard_map/ppermute | solution.py:32

commit v4 on v3

--- a/solution.py
+++ b/solution.py
@@ -18,7 +18,7 @@
 clip_level = 4.0
 expo_levels = (-1, 0, 1, 2, 3)
 lanes = 128
-pieces = 2
+pieces = 4
 MESH = pl.DeviceIdType.MESH
 
 
@@ -171,7 +171,7 @@
 def mixer(x_in, b_group, c_group, cumul, step_size, skip):
     n = lax.axis_size("seq")
     rows, width = x_in.shape
-    tile = min(256, width)
+    tile = min(128, width)
     tiles = width // tile
     states = b_group.shape[1]
     vmem = pl.BlockSpec(memory_space=pltpu.VMEM)

time: 122 us -> 120 us (0.984)
  Pallas kernels: 92.9 us -> 90.5 us
    pallas_call x1, Pallas kernels: 62.2 us -> 59.7 us  [project(): pl.pallas_call(functools.partial(project_kernel, n, n_chan, n_sub, min(25...]
where the time goes in v4:
time: 120 us; the launch traced here: 119 us
  Pallas kernels  90.5 us (75%)
  waiting for transfers between devices  12.3 us (10%)
  local copies, waits for them, and re-layouts  8.92 us (7%)
  other arithmetic  5.81 us (5%)
  starting transfers between devices  1.63 us (1%)
    pallas_call x1, Pallas kernels, project(): pl.pallas_call(functools.partial(project_kernel, n, n_chan, n_sub, min(25...  59.7 us
    pallas_call x1, Pallas kernels, mixer(): pl.pallas_call(functools.partial(mixer_kernel, n, tile), out_shape=jax.Sh...  28.1 us
    ppermute x2, waiting for transfers between devices, partner_2(): return lax.ppermute(block, axis, route)  12.3 us
    unnamed x17, local copies, waits for them, and re-layouts  5.46 us
    pallas_call x1, Pallas kernels, rotate(): pl.pallas_call(functools.partial(rotate_kernel, 1.0 / math.sqrt(LOCAL_HEA...  2.68 us
  transfers between devices with their start and end apart: 2, of which 2 were waited for; matrix products, arithmetic and copies ran while one was open for 2% of the time, Pallas kernels for 0%

profile of v4, /device:TPU:0, one launch (start us, length us, event | category | flops | bytes accessed | tf_op | source)
XLA Modules:
  0.0 119.3 jit_solution(17744280444626624025)
XLA Ops:
  0.0 1.2 %constant_dynamic-slice_fusion = (bf16[128,1,256]{2,1,0:T(2,128)(2,1)S(1)}, bf16[128,1,256]{2,1,0:T(2,128)(2,1)S(1)}) fusion(bf16[128,2,256]{2,1,0:T(2,128)(2,1)} %param.13, s32[]{:T(128)S(6)} %select_n.288, bf16[128,2,256]{2,1,0:T(2,128)(2,1)} %param.12), kind=kLoop, calls=%fused_computation.83 | loop fusion | bytes 262148 | tf_op jit(solution)/shard_map/dynamic_slice | solution.py:478
  1.2 0.1 copy.27
  1.4 0.8 copy.29
  2.2 0.2 reduce_window_sum.11.cum_ref
  2.4 0.1 copy.30
  2.4 0.8 copy.31.step_ref
  3.3 0.7 broadcast_in_dim.70
  4.0 0.1 broadcast_in_dim_reshape.3.skip_ref
  4.1 1.0 copy-done
  5.1 0.7 copy-done.1
  5.9 28.1 %shard_map.109 = f32[128,2048]{1,0:T(8,128)S(1)} custom-call(bf16[128,2048]{1,0:T(8,128)(2,1)S(1)} %copy-done, bf16[256,128]{1,0:T(8,128)(2,1)S(1)} %bitcast.12, bf16[128,256]{1,0:T(8,128)(2,1)S(1)} %bitcast.13, f32[128,32]{1,0:T(8,128)S(1)} %reduce_window_sum.11.cum_ref, f32[128,32]{1,0:T(8,128)S(1)} %copy.31.step_ref, f32[32,128]{1,0:T(8,128)S(1)} %bitcast.15, ...), custom_call_target="tpu_custom_call" | custom-call | tf_op jit(solution)/shard_map/pallas_call | solution.py:178
  34.0 0.0 copy-start.4
  34.0 0.0 copy-start.3
  34.0 1.3 %fusion.25 = f32[128,2048]{1,0:T(8,128)S(1)} fusion(f32[128,2048]{1,0:T(8,128)S(1)} %shard_map.109, bf16[128,2048]{1,0:T(8,128)(2,1)} %param.17), kind=kLoop, calls=%fused_computation.85 | loop fusion | flops 1835008 | bytes 2621440 | tf_op jit(solution)/shard_map/mul | solution.py:482
  35.3 0.9 mul.142
  36.2 0.0 copy-start.2
  36.2 0.3 reduce_sum.9
  36.6 0.3 mul.143
  37.0 0.3 copy.35
  37.4 0.4 fusion.7
  37.8 0.1 collective-permute-start
  37.9 0.6 fusion.17
  38.5 1.2 %collective-permute-done = bf16[128,2048]{1,0:T(8,128)(2,1)S(1)} collective-permute-done((bf16[128,2048]{1,0:T(8,128)(2,1)S(1)}, bf16[128,2048]{1,0:T(8,128)(2,1)S(1)}, u32[]{:S(2)}, u32[]{:S(2)}) %collective-permute-start) | collective-permute-done | bytes 524320 | tf_op jit(solution)/shard_map/ppermute | solution.py:32
  39.7 0.2 fusion.6
  39.9 1.6 %collective-permute-start.1 = (bf16[128,2048]{1,0:T(8,128)(2,1)S(1)}, bf16[128,2048]{1,0:T(8,128)(2,1)S(1)}, u32[]{:S(2)}, u32[]{:S(2)}) collective-permute-start(bf16[128,2048]{1,0:T(8,128)(2,1)S(1)} %fusion.6), channel_id=1, source_target_pairs={{0,2},{2,0},{1,3},{3,1},{4,6},{6,4},{5,7},{7,5},{8,10},{10,8},{9,1... | collective-permute-start | bytes 1572872 | tf_op jit(solution)/shard_map/ppermute | solution.py:32
  41.5 0.6 fusion.14
  42.1 0.8 fusion.11.table_ref
  42.9 11.0 %collective-permute-done.1 = bf16[128,2048]{1,0:T(8,128)(2,1)S(1)} collective-permute-done((bf16[128,2048]{1,0:T(8,128)(2,1)S(1)}, bf16[128,2048]{1,0:T(8,128)(2,1)S(1)}, u32[]{:S(2)}, u32[]{:S(2)}) %collective-permute-start.1) | collective-permute-done | bytes 524320 | tf_op jit(solution)/shard_map/ppermute | solution.py:32
  54.0 1.3 %fusion.5.mixed_ref = f32[128,2048]{1,0:T(8,128)} fusion(bf16[128,2048]{1,0:T(8,128)(2,1)S(1)} %collective-permute-done.1, bf16[128,2048]{1,0:T(8,128)(2,1)S(1)} %fusion.7, bf16[128,2048]{1,0:T(8,128)(2,1)S(1)} %collective-permute-done, pred[]{:T(512)S(6)} %eq.51, pred[]{:T(512)S(6)} %eq.50), kind=kLoop, calls=%fused_computation.11 | loop fusion | flops 2359296 | bytes 2621442 | tf_op jit(solution)/shard_map/jit(_where)/select_n | solution.py:496
  55.2 2.7 %shard_map.110.scaled_ref = bf16[128,2048]{1,0:T(8,128)(2,1)} custom-call(f32[128,2048]{1,0:T(8,128)} %fusion.5.mixed_ref, bf16[128,128]{1,0:T(8,128)(2,1)} %fusion.11.table_ref, f32[1,2048]{1,0:T(1,128)} %bitcast.19, f32[1,2048]{1,0:T(1,128)} %bitcast.18), custom_call_target="tpu_custom_call" | custom-call | tf_op jit(solution)/shard_map/pallas_call | solution.py:226
  57.9 59.7 %shard_map.111 = bf16[32,4096]{1,0:T(8,128)(2,1)} custom-call(bf16[128,2048]{1,0:T(8,128)(2,1)} %shard_map.110.scaled_ref, bf16[2048,1024]{1,0:T(8,128)(2,1)} %weight_hbm.1), custom_call_target="tpu_custom_call" | custom-call | tf_op jit(solution)/shard_map/pallas_call | solution.py:433
  117.6 1.7 %copy.40 = bf16[32,4096]{1,0:T(8,128)(2,1)} copy(bf16[32,4096]{1,0:T(8,128)(2,1)} %shard_map.111) | data formatting | bytes 524288
  (14 shorter events, 0.1 us)
Async XLA Ops:
  4.1 1.0 copy-start
  5.1 0.7 copy-start.1
  34.0 3.4 %copy-start.4 = (s32[2048]{0:T(1024)S(1)}, s32[2048]{0:T(1024)}, u32[]{:S(2)}) copy-start(s32[2048]{0:T(1024)} %param.19) | copy-start | bytes 24580
  34.0 3.4 %copy-start.3 = (f32[2048]{0:T(1024)S(1)}, f32[2048]{0:T(1024)}, u32[]{:S(2)}) copy-start(f32[2048]{0:T(1024)} %param.18) | copy-start | bytes 24580
  36.2 1.1 copy-start.2
  36.2 1.7 %copy-start.5 = (s32[2048]{0:T(1024)S(1)}, s32[2048]{0:T(1024)}, u32[]{:S(2)}) copy-start(s32[2048]{0:T(1024)} %param.20) | copy-start | bytes 24580
  37.8 2.0 %collective-permute-start = (bf16[128,2048]{1,0:T(8,128)(2,1)S(1)}, bf16[128,2048]{1,0:T(8,128)(2,1)S(1)}, u32[]{:S(2)}, u32[]{:S(2)}) collective-permute-start(bf16[128,2048]{1,0:T(8,128)(2,1)S(1)} %fusion.7), channel_id=1, source_target_pairs={{0,1},{1,0},{2,3},{3,2},{4,5},{5,4},{6,7},{7,6},{8,9},{9,8},{10,11... | collective-permute-start | bytes 1572872 | tf_op jit(solution)/shard_map/ppermute | solution.py:32
  39.9 14.0 %collective-permute-start.1 = (bf16[128,2048]{1,0:T(8,128)(2,1)S(1)}, bf16[128,2048]{1,0:T(8,128)(2,1)S(1)}, u32[]{:S(2)}, u32[]{:S(2)}) collective-permute-start(bf16[128,2048]{1,0:T(8,128)(2,1)S(1)} %fusion.6), channel_id=1, source_target_pairs={{0,2},{2,0},{1,3},{3,1},{4,6},{6,4},{5,7},{7,5},{8,10},{10,8},{9,1... | collective-permute-start | bytes 1572872 | tf_op jit(solution)/shard_map/ppermute | solution.py:32

commit v5 on v4

--- a/solution.py
+++ b/solution.py
@@ -282,9 +282,9 @@
 
     piece = slots.shape[1] // pieces
 
-    def hop(k, q, way):
+    def hop(k, q, way, source=None):
         return pltpu.make_async_remote_copy(
-            src_ref=slots.at[k, pl.ds(q * piece, piece)],
+            src_ref=(slots.at[k] if source is None else source).at[pl.ds(q * piece, piece)],
             dst_ref=slots.at[k, pl.ds(q * piece, piece)],
             send_sem=g_send.at[way, k, q],
             recv_sem=g_recv.at[k, q],
@@ -316,20 +316,20 @@
     def when_valid(k, act):
         pl.when(jnp.logical_and(k >= 0, k < n))(lambda: act(k))
 
-    def to_right(k, q):
+    def to_right(k, q, source=None):
         @pl.when(me + 1 < n)
         def _():
-            hop(k, q, 1).start()
-
-    def to_left(k, q):
+            hop(k, q, 1, source).start()
+
+    def to_left(k, q, source=None):
         @pl.when(me > 0)
         def _():
-            hop(k, q, 0).start()
-
+            hop(k, q, 0, source).start()
+
+    for q in range(pieces):
+        to_right(me, q, scaled_ref)
+        to_left(me, q, scaled_ref)
     own.wait()
-    for q in range(pieces):
-        to_right(me, q)
-        to_left(me, q)
     fetch.wait()
 
     def project_block(k):

time: 120 us -> 120 us (level)
  no operation moved by 1% of the time
where the time goes in v5:
time: 120 us; the launch traced here: 119 us
  Pallas kernels  90.5 us (75%)
  waiting for transfers between devices  12.3 us (10%)
  local copies, waits for them, and re-layouts  8.92 us (7%)
  other arithmetic  5.81 us (5%)
  starting transfers between devices  1.63 us (1%)
    pallas_call x1, Pallas kernels, project(): pl.pallas_call(functools.partial(project_kernel, n, n_chan, n_sub, min(25...  59.7 us
    pallas_call x1, Pallas kernels, mixer(): pl.pallas_call(functools.partial(mixer_kernel, n, tile), out_shape=jax.Sh...  28.1 us
    ppermute x2, waiting for transfers between devices, partner_2(): return lax.ppermute(block, axis, route)  12.3 us
    unnamed x17, local copies, waits for them, and re-layouts  5.46 us
    pallas_call x1, Pallas kernels, rotate(): pl.pallas_call(functools.partial(rotate_kernel, 1.0 / math.sqrt(LOCAL_HEA...  2.68 us
  transfers between devices with their start and end apart: 2, of which 2 were waited for; matrix products, arithmetic and copies ran while one was open for 2% of the time, Pallas kernels for 0%

profile of v5, /device:TPU:0, one launch (start us, length us, event | category | flops | bytes accessed | tf_op | source)
XLA Modules:
  0.0 119.3 jit_solution(4316568772709491757)
XLA Ops:
  0.0 1.2 %constant_dynamic-slice_fusion = (bf16[128,1,256]{2,1,0:T(2,128)(2,1)S(1)}, bf16[128,1,256]{2,1,0:T(2,128)(2,1)S(1)}) fusion(bf16[128,2,256]{2,1,0:T(2,128)(2,1)} %param.13, s32[]{:T(128)S(6)} %select_n.288, bf16[128,2,256]{2,1,0:T(2,128)(2,1)} %param.12), kind=kLoop, calls=%fused_computation.83 | loop fusion | bytes 262148 | tf_op jit(solution)/shard_map/dynamic_slice | solution.py:478
  1.2 0.1 copy.27
  1.4 0.8 copy.29
  2.2 0.2 reduce_window_sum.11.cum_ref
  2.4 0.1 copy.30
  2.4 0.8 copy.31.step_ref
  3.3 0.7 broadcast_in_dim.70
  4.0 0.1 broadcast_in_dim_reshape.3.skip_ref
  4.1 1.0 copy-done
  5.1 0.7 copy-done.1
  5.9 28.1 %shard_map.109 = f32[128,2048]{1,0:T(8,128)S(1)} custom-call(bf16[128,2048]{1,0:T(8,128)(2,1)S(1)} %copy-done, bf16[256,128]{1,0:T(8,128)(2,1)S(1)} %bitcast.12, bf16[128,256]{1,0:T(8,128)(2,1)S(1)} %bitcast.13, f32[128,32]{1,0:T(8,128)S(1)} %reduce_window_sum.11.cum_ref, f32[128,32]{1,0:T(8,128)S(1)} %copy.31.step_ref, f32[32,128]{1,0:T(8,128)S(1)} %bitcast.15, ...), custom_call_target="tpu_custom_call" | custom-call | tf_op jit(solution)/shard_map/pallas_call | solution.py:178
  34.0 0.0 copy-start.4
  34.0 0.0 copy-start.3
  34.0 1.3 %fusion.25 = f32[128,2048]{1,0:T(8,128)S(1)} fusion(f32[128,2048]{1,0:T(8,128)S(1)} %shard_map.109, bf16[128,2048]{1,0:T(8,128)(2,1)} %param.17), kind=kLoop, calls=%fused_computation.85 | loop fusion | flops 1835008 | bytes 2621440 | tf_op jit(solution)/shard_map/mul | solution.py:482
  35.3 0.9 mul.142
  36.2 0.0 copy-start.2
  36.2 0.3 reduce_sum.9
  36.6 0.3 mul.143
  37.0 0.3 copy.35
  37.4 0.4 fusion.7
  37.8 0.1 collective-permute-start
  37.9 0.6 fusion.17
  38.5 1.2 %collective-permute-done = bf16[128,2048]{1,0:T(8,128)(2,1)S(1)} collective-permute-done((bf16[128,2048]{1,0:T(8,128)(2,1)S(1)}, bf16[128,2048]{1,0:T(8,128)(2,1)S(1)}, u32[]{:S(2)}, u32[]{:S(2)}) %collective-permute-start) | collective-permute-done | bytes 524320 | tf_op jit(solution)/shard_map/ppermute | solution.py:32
  39.7 0.2 fusion.6
  39.9 1.6 %collective-permute-start.1 = (bf16[128,2048]{1,0:T(8,128)(2,1)S(1)}, bf16[128,2048]{1,0:T(8,128)(2,1)S(1)}, u32[]{:S(2)}, u32[]{:S(2)}) collective-permute-start(bf16[128,2048]{1,0:T(8,128)(2,1)S(1)} %fusion.6), channel_id=1, source_target_pairs={{0,2},{2,0},{1,3},{3,1},{4,6},{6,4},{5,7},{7,5},{8,10},{10,8},{9,1... | collective-permute-start | bytes 1572872 | tf_op jit(solution)/shard_map/ppermute | solution.py:32
  41.5 0.6 fusion.14
  42.1 0.8 fusion.11.table_ref
  42.9 11.0 %collective-permute-done.1 = bf16[128,2048]{1,0:T(8,128)(2,1)S(1)} collective-permute-done((bf16[128,2048]{1,0:T(8,128)(2,1)S(1)}, bf16[128,2048]{1,0:T(8,128)(2,1)S(1)}, u32[]{:S(2)}, u32[]{:S(2)}) %collective-permute-start.1) | collective-permute-done | bytes 524320 | tf_op jit(solution)/shard_map/ppermute | solution.py:32
  54.0 1.3 %fusion.5.mixed_ref = f32[128,2048]{1,0:T(8,128)} fusion(bf16[128,2048]{1,0:T(8,128)(2,1)S(1)} %collective-permute-done.1, bf16[128,2048]{1,0:T(8,128)(2,1)S(1)} %fusion.7, bf16[128,2048]{1,0:T(8,128)(2,1)S(1)} %collective-permute-done, pred[]{:T(512)S(6)} %eq.51, pred[]{:T(512)S(6)} %eq.50), kind=kLoop, calls=%fused_computation.11 | loop fusion | flops 2359296 | bytes 2621442 | tf_op jit(solution)/shard_map/jit(_where)/select_n | solution.py:496
  55.2 2.7 %shard_map.110.scaled_ref = bf16[128,2048]{1,0:T(8,128)(2,1)} custom-call(f32[128,2048]{1,0:T(8,128)} %fusion.5.mixed_ref, bf16[128,128]{1,0:T(8,128)(2,1)} %fusion.11.table_ref, f32[1,2048]{1,0:T(1,128)} %bitcast.19, f32[1,2048]{1,0:T(1,128)} %bitcast.18), custom_call_target="tpu_custom_call" | custom-call | tf_op jit(solution)/shard_map/pallas_call | solution.py:226
  57.9 59.7 %shard_map.111 = bf16[32,4096]{1,0:T(8,128)(2,1)} custom-call(bf16[128,2048]{1,0:T(8,128)(2,1)} %shard_map.110.scaled_ref, bf16[2048,1024]{1,0:T(8,128)(2,1)} %weight_hbm.1), custom_call_target="tpu_custom_call" | custom-call | tf_op jit(solution)/shard_map/pallas_call | solution.py:433
  117.6 1.7 %copy.40 = bf16[32,4096]{1,0:T(8,128)(2,1)} copy(bf16[32,4096]{1,0:T(8,128)(2,1)} %shard_map.111) | data formatting | bytes 524288
  (14 shorter events, 0.1 us)
Async XLA Ops:
  4.1 1.0 copy-start
  5.1 0.7 copy-start.1
  34.0 3.4 %copy-start.4 = (s32[2048]{0:T(1024)S(1)}, s32[2048]{0:T(1024)}, u32[]{:S(2)}) copy-start(s32[2048]{0:T(1024)} %param.19) | copy-start | bytes 24580
  34.0 3.4 %copy-start.3 = (f32[2048]{0:T(1024)S(1)}, f32[2048]{0:T(1024)}, u32[]{:S(2)}) copy-start(f32[2048]{0:T(1024)} %param.18) | copy-start | bytes 24580
  36.2 1.1 copy-start.2
  36.2 1.7 %copy-start.5 = (s32[2048]{0:T(1024)S(1)}, s32[2048]{0:T(1024)}, u32[]{:S(2)}) copy-start(s32[2048]{0:T(1024)} %param.20) | copy-start | bytes 24580
  37.8 2.0 %collective-permute-start = (bf16[128,2048]{1,0:T(8,128)(2,1)S(1)}, bf16[128,2048]{1,0:T(8,128)(2,1)S(1)}, u32[]{:S(2)}, u32[]{:S(2)}) collective-permute-start(bf16[128,2048]{1,0:T(8,128)(2,1)S(1)} %fusion.7), channel_id=1, source_target_pairs={{0,1},{1,0},{2,3},{3,2},{4,5},{5,4},{6,7},{7,6},{8,9},{9,8},{10,11... | collective-permute-start | bytes 1572872 | tf_op jit(solution)/shard_map/ppermute | solution.py:32
  39.9 14.0 %collective-permute-start.1 = (bf16[128,2048]{1,0:T(8,128)(2,1)S(1)}, bf16[128,2048]{1,0:T(8,128)(2,1)S(1)}, u32[]{:S(2)}, u32[]{:S(2)}) collective-permute-start(bf16[128,2048]{1,0:T(8,128)(2,1)S(1)} %fusion.6), channel_id=1, source_target_pairs={{0,2},{2,0},{1,3},{3,1},{4,6},{6,4},{5,7},{7,5},{8,10},{10,8},{9,1... | collective-permute-start | bytes 1572872 | tf_op jit(solution)/shard_map/ppermute | solution.py:32
